TPU v7x, 256 devices: a whole 4x4x8 slice. The times are simulated.
256 devices in a mesh: stream: 16 (over y, x), span: 16 (over z, core).
Axes of the slice: x: 4, y: 4, z: 8, core: 2. Of those that a mesh axis runs over, the one named last changes fastest.
Arguments:
- species: float32 [9, 128, 16, 2048], P(None, 'stream', None, 'span'), may hold values from -6 to 6
- history: float32 [16, 16, 32, 3, 9, 128], P('stream', 'span'), may hold values from -6 to 6
- flame_tiles: int32 [16, 16, 32], P('stream', 'span'), may hold values from 0 to 127, as said below
- owners: int32 [16, 16, 32, 1], P('stream', 'span'), may hold values from 0 to 15, as said below
- orders: int32 [16, 16, 32], P('stream', 'span'), may hold values from 1 to 3
- substeps: int32 [16, 16, 32], P('stream', 'span'), may hold values from 1 to 8
- levels: int32 [128, 16, 16], P('stream', None, 'span'), may hold values from 0 to 3
- mechanism: float32 [9, 9], replicated, may hold values from -2 to 2
Outputs:
- species_next: float32 [9, 128, 16, 2048], P(None, 'stream', None, 'span')
- chem_load: int32 [16, 16], P('stream', 'span')
Inputs may be any that keep to these rules, and one draw needn't show every extreme that they name: `flame_tiles`: within one device's list the tile indices are distinct. `owners`: among the flame tiles of one device, no owner is named more than 6 times, and some owner exactly 6 times.
All inputs are finite; a program needn't handle non-finite values.
Results may differ from a plain program's by a relative error of at most 0.0003.
Values sent between devices are 32-bit elements; how exact they have to be, the bound alone decides.
A program may use at most 64 MiB of HBM per device.

v0:
```python
import jax
import jax.numpy as jnp
from jax import lax
from jax.sharding import PartitionSpec as P

SUBMAX = 8


def cut_along(array, dim, devices):
    before, after = (array.shape[:dim], array.shape[dim + 1 :])
    return jnp.moveaxis(array.reshape(*before, devices, -1, *after), dim, 0)


def sum_at_owner(array, axis, dim):
    pieces = cut_along(array, dim, lax.axis_size(axis))
    arrived = lax.all_to_all(pieces, axis, split_axis=0, concat_axis=0, tiled=True)
    return arrived.sum(axis=0)


def extended(array, sides, width):
    edges = {}
    for axis, dim in sides:
        devices, length = (lax.axis_size(axis), array.shape[dim])
        up = [(i, (i + 1) % devices) for i in range(devices - 1)]
        last = lax.slice_in_dim(array, length - width, length, axis=dim)
        initial = lax.slice_in_dim(array, 0, width, axis=dim)
        edges[dim] = (
            lax.ppermute(last, axis, up),
            lax.ppermute(initial, axis, [(b, a) for a, b in up]),
        )
    done = []
    for _, dim in sides:
        low, high = edges[dim]
        around = [(width, width) if d in done else (0, 0) for d in range(array.ndim)]
        array = jnp.concatenate([jnp.pad(low, around), array, jnp.pad(high, around)], axis=dim)
        done.append(dim)
    return array


def bdf_tables(order):
    level_ids = jnp.arange(1, 4, dtype=jnp.int32)
    selector = (order[:, None] == level_ids[None, :]).astype(jnp.float32)
    predictor_table = jnp.array([[1.0, 0.0, 0.0], [2.0, -1.0, 0.0], [3.0, -3.0, 1.0]], jnp.float32)
    corrector_table = jnp.array(
        [[1.0, 0.0, 0.0], [4.0 / 3.0, -1.0 / 3.0, 0.0], [18.0 / 11.0, -9.0 / 11.0, 2.0 / 11.0]],
        jnp.float32,
    )
    beta_table = jnp.array([1.0, 2.0 / 3.0, 6.0 / 11.0], jnp.float32)
    high = lax.Precision.HIGHEST
    return (
        jnp.dot(selector, predictor_table, precision=high),
        jnp.dot(selector, corrector_table, precision=high),
        jnp.dot(selector, beta_table, precision=high),
    )


def integrate(history, order, substeps, mechanism):
    high = lax.Precision.HIGHEST
    predictor, corrector, beta = bdf_tables(order)
    initial = history[:, 0]
    for substep_index in range(SUBMAX):
        guess = jnp.einsum("km,kmsc->ksc", predictor, history, precision=high)
        force = jnp.tanh(jnp.einsum("st,ktc->ksc", mechanism, guess, precision=high))
        fresh = (
            jnp.einsum("km,kmsc->ksc", corrector, history, precision=high)
            + 0.5 * beta[:, None, None] * force
        )
        moved = jnp.stack([fresh, history[:, 0], history[:, 1]], axis=1)
        active = (substeps > substep_index)[:, None, None, None]
        history = jnp.where(active, moved, history)
    divisor = jnp.maximum(substeps.astype(jnp.float32), 1.0)
    return (history[:, 0] - initial) / divisor[:, None, None]


def gauss_table(length, width):
    position = jnp.arange(length, dtype=jnp.float32)
    offset = (position[:, None] - position[None, :]) / width
    kernel = jnp.exp(-0.5 * offset * offset)
    return kernel / jnp.sum(kernel, axis=1, keepdims=True)


def sensor_of(rates):
    power = jnp.mean(rates * rates, axis=0, keepdims=True)
    return power / (power + 1.0)


def shards(species, history, flame_tiles, owners, orders, substeps, levels, mechanism):
    n_species, z_cells, x_cells, y_cells = species.shape
    span_count = lax.axis_size("span")
    tile_index = flame_tiles.reshape(-1)
    owner_list = owners.reshape(-1)
    order_list = orders.reshape(-1)
    step_list = substeps.reshape(-1)
    local_history = history.reshape(history.shape[2:])
    owner_ids = jnp.arange(span_count, dtype=jnp.int32)
    owned = (owner_list[:, None] == owner_ids[None, :]).astype(jnp.int32)
    tile_rate = integrate(local_history, order_list, step_list, mechanism)
    shares = jnp.sum(owned.astype(jnp.float32) * step_list.astype(jnp.float32)[:, None], axis=0)
    load_value = sum_at_owner(shares, "span", 0)[0].astype(jnp.int32)
    placed = jnp.zeros((n_species, z_cells * x_cells, y_cells), jnp.float32)
    placed = placed.at[:, tile_index, :].set(jnp.transpose(tile_rate, (1, 0, 2)))
    rates = placed.reshape((n_species, z_cells, x_cells, y_cells))
    rows = lax.all_to_all(rates, "stream", split_axis=2, concat_axis=1, tiled=True)
    finish_rows = jnp.concatenate([rows, sensor_of(rows)], axis=0)
    table = gauss_table(finish_rows.shape[1], 2.0 * z_cells)
    smoothed = jnp.einsum("zk,rkxy->rzxy", table, finish_rows, precision=lax.Precision.HIGHEST)
    filtered = lax.all_to_all(smoothed, "stream", split_axis=1, concat_axis=2, tiled=True)
    fine_rates = filtered[:n_species]
    fine_sensor = filtered[n_species]
    class_ids = jnp.arange(4, dtype=jnp.int32)
    peak_values = jnp.array([2.5, 5.0, 10.0, 20.0], jnp.float32)
    peak = jnp.sum(jnp.where(levels[..., None] == class_ids, peak_values, 0.0), axis=-1)
    thick = 1.0 + (peak - 1.0) * fine_sensor
    padded = extended(species, (("stream", 1), ("span", 3)), 1)
    padded = jnp.pad(padded, ((0, 0), (0, 0), (1, 1), (0, 0)))
    beside_all = padded[:, 2:, 1:-1, 1:-1] + padded[:, :-2, 1:-1, 1:-1]
    beside_all = beside_all + padded[:, 1:-1, 2:, 1:-1] + padded[:, 1:-1, :-2, 1:-1]
    beside_all = beside_all + padded[:, 1:-1, 1:-1, 2:] + padded[:, 1:-1, 1:-1, :-2]
    spread = beside_all - 6.0 * species
    species_next = species + 0.02 * thick * spread + 4.0 * fine_rates / thick
    return (species_next, load_value.reshape((1, 1)))


def solution(mesh):
    in_specs = (
        P(None, "stream", None, "span"),
        P("stream", "span", None, None, None, None),
        P("stream", "span", None),
        P("stream", "span", None, None),
        P("stream", "span", None),
        P("stream", "span", None),
        P("stream", None, "span"),
        P(),
    )
    out_specs = (P(None, "stream", None, "span"), P("stream", "span"))
    return jax.shard_map(shards, mesh=mesh, in_specs=in_specs, out_specs=out_specs, check_vma=False)
```

profile of v0, /device:TPU:1, one launch (start us, length us, event | category | flops | bytes accessed | tf_op | source)
XLA Modules:
  0.0 104.3 jit_solution(3827058442761338248)
XLA Ops:
  2.6 2.4 %fusion.64 = f32[32,1,9,128]{3,1,2,0:T(1,128)S(1)} fusion(f32[32,3,1,1]{1,2,3,0:T(1,128)S(1)} %bitcast.235, f32[32,3,9,128]{3,0,2,1:T(8,128)} %bitcast.228), kind=kOutput, calls=%fused_computation.83 | convolution fusion | flops 1327104 | bytes 590208 | tf_op jit(solution)/shard_map/km,kmsc->ksc/dot_general | solution.py:62
  5.9 2.4 %fusion.66 = f32[32,1,9,128]{3,1,2,0:T(1,128)S(1)} fusion(f32[32,3,1,1]{1,2,3,0:T(1,128)S(1)} %bitcast.243, f32[32,3,9,128]{3,0,2,1:T(8,128)} %bitcast.229), kind=kOutput, calls=%fused_computation.85 | convolution fusion | flops 1327104 | bytes 590208 | tf_op jit(solution)/shard_map/km,kmsc->ksc/dot_general | solution.py:65
  9.8 1.4 %fusion.60 = f32[32,1,9,128]{3,1,2,0:T(1,128)S(1)} fusion(f32[32,3,1,1]{1,2,3,0:T(1,128)S(1)} %bitcast.236, f32[32,3,9,128]{3,0,2,1:T(8,128)S(1)} %maximum_select_fusion), kind=kOutput, calls=%fused_computation.79 | convolution fusion | flops 1327104 | bytes 590208 | tf_op jit(solution)/shard_map/km,kmsc->ksc/dot_general | solution.py:62
  11.2 1.4 %fusion.62 = f32[32,1,9,128]{3,1,2,0:T(1,128)S(1)} fusion(f32[32,3,1,1]{1,2,3,0:T(1,128)S(1)} %bitcast.244, f32[32,3,9,128]{3,0,2,1:T(8,128)S(1)} %maximum_select_fusion), kind=kOutput, calls=%fused_computation.81 | convolution fusion | flops 1327104 | bytes 590208 | tf_op jit(solution)/shard_map/km,kmsc->ksc/dot_general | solution.py:65
  13.2 1.4 %fusion.56 = f32[32,1,9,128]{3,1,2,0:T(1,128)S(1)} fusion(f32[32,3,1,1]{1,2,3,0:T(1,128)S(1)} %bitcast.237, f32[32,3,9,128]{3,0,2,1:T(8,128)S(1)} %maximum_select_fusion.1), kind=kOutput, calls=%fused_computation.75 | convolution fusion | flops 1327104 | bytes 590208 | tf_op jit(solution)/shard_map/km,kmsc->ksc/dot_general | solution.py:62
  14.6 1.4 %fusion.58 = f32[32,1,9,128]{3,1,2,0:T(1,128)S(1)} fusion(f32[32,3,1,1]{1,2,3,0:T(1,128)S(1)} %bitcast.245, f32[32,3,9,128]{3,0,2,1:T(8,128)S(1)} %maximum_select_fusion.1), kind=kOutput, calls=%fused_computation.77 | convolution fusion | flops 1327104 | bytes 590208 | tf_op jit(solution)/shard_map/km,kmsc->ksc/dot_general | solution.py:65
  16.6 1.4 %fusion.52 = f32[32,1,9,128]{3,1,2,0:T(1,128)S(1)} fusion(f32[32,3,1,1]{1,2,3,0:T(1,128)S(1)} %bitcast.238, f32[32,3,9,128]{3,0,2,1:T(8,128)S(1)} %maximum_select_fusion.2), kind=kOutput, calls=%fused_computation.71 | convolution fusion | flops 1327104 | bytes 590208 | tf_op jit(solution)/shard_map/km,kmsc->ksc/dot_general | solution.py:62
  18.0 1.6 %fusion.54 = f32[32,1,9,128]{3,1,2,0:T(1,128)S(1)} fusion(f32[32,3,1,1]{1,2,3,0:T(1,128)S(1)} %bitcast.246, f32[32,3,9,128]{3,0,2,1:T(8,128)S(1)} %maximum_select_fusion.2), kind=kOutput, calls=%fused_computation.73 | convolution fusion | flops 1327104 | bytes 590208 | tf_op jit(solution)/shard_map/km,kmsc->ksc/dot_general | solution.py:65
  20.2 1.4 %fusion.48 = f32[32,1,9,128]{3,1,2,0:T(1,128)S(1)} fusion(f32[32,3,1,1]{1,2,3,0:T(1,128)S(1)} %bitcast.239, f32[32,3,9,128]{3,0,2,1:T(8,128)S(1)} %maximum_select_fusion.3), kind=kOutput, calls=%fused_computation.67 | convolution fusion | flops 1327104 | bytes 590208 | tf_op jit(solution)/shard_map/km,kmsc->ksc/dot_general | solution.py:62
  21.6 1.4 %fusion.50 = f32[32,1,9,128]{3,1,2,0:T(1,128)S(1)} fusion(f32[32,3,1,1]{1,2,3,0:T(1,128)S(1)} %bitcast.247, f32[32,3,9,128]{3,0,2,1:T(8,128)S(1)} %maximum_select_fusion.3), kind=kOutput, calls=%fused_computation.69 | convolution fusion | flops 1327104 | bytes 590208 | tf_op jit(solution)/shard_map/km,kmsc->ksc/dot_general | solution.py:65
  23.6 1.4 %fusion.44 = f32[32,1,9,128]{3,1,2,0:T(1,128)S(1)} fusion(f32[32,3,1,1]{1,2,3,0:T(1,128)S(1)} %bitcast.240, f32[32,3,9,128]{3,0,2,1:T(8,128)S(1)} %maximum_select_fusion.4), kind=kOutput, calls=%fused_computation.63 | convolution fusion | flops 1327104 | bytes 590208 | tf_op jit(solution)/shard_map/km,kmsc->ksc/dot_general | solution.py:62
  25.0 1.4 %fusion.46 = f32[32,1,9,128]{3,1,2,0:T(1,128)S(1)} fusion(f32[32,3,1,1]{1,2,3,0:T(1,128)S(1)} %bitcast.248, f32[32,3,9,128]{3,0,2,1:T(8,128)S(1)} %maximum_select_fusion.4), kind=kOutput, calls=%fused_computation.65 | convolution fusion | flops 1327104 | bytes 590208 | tf_op jit(solution)/shard_map/km,kmsc->ksc/dot_general | solution.py:65
  27.0 1.4 %fusion.40 = f32[32,1,9,128]{3,1,2,0:T(1,128)S(1)} fusion(f32[32,3,1,1]{1,2,3,0:T(1,128)S(1)} %bitcast.241, f32[32,3,9,128]{3,0,2,1:T(8,128)S(1)} %maximum_select_fusion.5), kind=kOutput, calls=%fused_computation.59 | convolution fusion | flops 1327104 | bytes 590208 | tf_op jit(solution)/shard_map/km,kmsc->ksc/dot_general | solution.py:62
  28.4 1.4 %fusion.42 = f32[32,1,9,128]{3,1,2,0:T(1,128)S(1)} fusion(f32[32,3,1,1]{1,2,3,0:T(1,128)S(1)} %bitcast.249, f32[32,3,9,128]{3,0,2,1:T(8,128)S(1)} %maximum_select_fusion.5), kind=kOutput, calls=%fused_computation.61 | convolution fusion | flops 1327104 | bytes 590208 | tf_op jit(solution)/shard_map/km,kmsc->ksc/dot_general | solution.py:65
  30.6 1.4 %fusion.36 = f32[32,1,9,128]{3,1,2,0:T(1,128)S(1)} fusion(f32[32,3,1,1]{1,2,3,0:T(1,128)S(1)} %bitcast.242, f32[32,3,9,128]{3,0,2,1:T(8,128)S(1)} %maximum_select_fusion.6), kind=kOutput, calls=%fused_computation.55 | convolution fusion | flops 1327104 | bytes 590208 | tf_op jit(solution)/shard_map/km,kmsc->ksc/dot_general | solution.py:62
  32.0 1.4 %fusion.38 = f32[32,1,9,128]{3,1,2,0:T(1,128)S(1)} fusion(f32[32,3,1,1]{1,2,3,0:T(1,128)S(1)} %bitcast.250, f32[32,3,9,128]{3,0,2,1:T(8,128)S(1)} %maximum_select_fusion.6), kind=kOutput, calls=%fused_computation.57 | convolution fusion | flops 1327104 | bytes 590208 | tf_op jit(solution)/shard_map/km,kmsc->ksc/dot_general | solution.py:65
  34.2 1.5 %scatter_fusion = f32[9,128,128]{2,0,1:T(8,128)S(1)} fusion(f32[9,128,128]{2,0,1:T(8,128)S(1)} %broadcast_in_dim.85, s32[32]{0:T(128)S(1)} %fusion.123, f32[32,9,128]{2,1,0:T(8,128)S(1)} %copy.116), kind=kCustom, calls=%fused_computation | custom fusion | bytes 442496 | tf_op jit(solution)/shard_map/scatter | solution.py:101
  35.7 1.2 %copy.117 = f32[9,8,16,128]{3,1,0,2:T(8,128)} copy(f32[9,8,16,128]{3,0,2,1:T(8,128)S(1)} %bitcast.231) | data formatting | bytes 1179648 | tf_op jit(solution)/shard_map/reshape | solution.py:102
  36.9 7.7 %all-to-all-start = ((f32[9,8,16,128]{3,1,0,2:T(8,128)}), f32[9,8,16,128]{3,1,0,2:T(8,128)S(1)}, u32[]{:S(2)}, u32[]{:S(2)}) async-start(f32[9,8,16,128]{3,1,0,2:T(8,128)} %copy.117), calls=%async_computation | async-start | bytes 1179648 | tf_op jit(solution)/shard_map/all_to_all | solution.py:103
  45.3 4.4 %collective-permute-start.2 = (f32[9,8,16,1]{2,1,3,0:T(8,128)S(1)}, f32[9,8,16,1]{2,1,3,0:T(8,128)S(1)}, u32[]{:S(2)}, u32[]{:S(2)}) collective-permute-start(f32[9,8,16,1]{2,1,3,0:T(8,128)S(1)} %copy.163), channel_id=1, source_target_pairs={{0,1},{1,2},{2,3},{3,4},{4,5},{5,6},{6,7},{7,8},{8,9},{9,10},{10,1... | collective-permute-start | bytes 13832 | tf_op jit(solution)/shard_map/ppermute | solution.py:28
  50.2 1.9 %collective-permute-start.3 = (f32[9,8,16,1]{2,1,3,0:T(8,128)S(1)}, f32[9,8,16,1]{2,1,3,0:T(8,128)}, u32[]{:S(2)}, u32[]{:S(2)}) collective-permute-start(f32[9,8,16,1]{2,1,3,0:T(8,128)S(1)} %copy.164), channel_id=1, source_target_pairs={{1,0},{2,1},{3,2},{4,3},{5,4},{6,5},{7,6},{8,7},{9,8},{10,9},{11,1... | collective-permute-start | bytes 13832 | tf_op jit(solution)/shard_map/ppermute | solution.py:29
  52.8 1.3 %collective-permute-start = (f32[9,1,16,128]{3,1,2,0:T(1,128)}, f32[9,1,16,128]{3,1,2,0:T(1,128)}, u32[]{:S(2)}, u32[]{:S(2)}) collective-permute-start(f32[9,1,16,128]{3,1,2,0:T(1,128)} %bitcast.65), channel_id=1, source_target_pairs={{16,0},{32,16},{48,32},{64,48},{80,64},{96,80},{112,96},{128,112},... | collective-permute-start | bytes 221192 | tf_op jit(solution)/shard_map/ppermute | solution.py:29
  54.1 4.8 %collective-permute-start.1 = (f32[9,1,16,128]{3,1,2,0:T(1,128)}, f32[9,1,16,128]{3,1,2,0:T(1,128)}, u32[]{:S(2)}, u32[]{:S(2)}) collective-permute-start(f32[9,1,16,128]{3,1,2,0:T(1,128)} %bitcast.66), channel_id=1, source_target_pairs={{0,16},{16,32},{32,48},{48,64},{64,80},{80,96},{96,112},{112,128},... | collective-permute-start | bytes 221192 | tf_op jit(solution)/shard_map/ppermute | solution.py:28
  59.8 10.3 %all-to-all-start.2 = ((f32[16,1,1]{2,1,0:T(1,128)}), f32[16,1,1]{2,1,0:T(1,128)S(1)}, u32[]{:S(2)}, u32[]{:S(2)}) async-start(f32[16,1,1]{2,1,0:T(1,128)} %copy.135), calls=%async_computation.2 | async-start | bytes 16384 | tf_op jit(solution)/shard_map/all_to_all | solution.py:16
  71.4 1.1 %copy.122 = f32[10,128,1,128]{3,2,0,1:T(1,128)} copy(f32[10,128,1,128]{1,3,0,2:T(8,128)S(1)} %convolution_bitcast_fusion) | data formatting | bytes 1310720 | tf_op jit(solution)/shard_map/zk,rkxy->rzxy/transpose | solution.py:106
  72.5 4.6 %all-to-all-done.2 = f32[16,1,1]{2,1,0:T(1,128)S(1)} async-done(((f32[16,1,1]{2,1,0:T(1,128)}), f32[16,1,1]{2,1,0:T(1,128)S(1)}, u32[]{:S(2)}, u32[]{:S(2)}) %all-to-all-start.2) | async-done | bytes 96 | tf_op jit(solution)/shard_map/all_to_all | solution.py:16
  77.2 8.2 %all-to-all-start.1 = ((f32[10,128,1,128]{3,2,0,1:T(1,128)}), f32[10,128,1,128]{3,2,0,1:T(1,128)}, u32[]{:S(2)}, u32[]{:S(2)}) async-start(f32[10,128,1,128]{3,2,0,1:T(1,128)} %copy.122), calls=%async_computation.1 | async-start | bytes 1310720 | tf_op jit(solution)/shard_map/all_to_all | solution.py:107
  87.7 1.3 %copy.132 = f32[9,8,16,1]{3,1,2,0:T(8,128)S(1)} copy(f32[9,8,16,1]{2,1,3,0:T(8,128)} %collective-permute-done.3) | data formatting | bytes 9216 | tf_op jit(solution)/shard_map/ppermute | solution.py:29
  89.1 4.1 %select_maximum_fusion = f32[9,10,18,130]{3,1,2,0:T(8,128)} fusion(f32[9,10,16,1]{3,1,2,0:T(8,128)S(1)} %pad.12, f32[9,10,16,1]{3,1,2,0:T(8,128)S(1)} %pad.11, f32[9,1,16,128]{3,1,2,0:T(1,128)} %collective-permute-done, f32[9,8,16,128]{3,1,2,0:T(8,128)S(1)} %copy.134, f32[9,1,16,128]{3,1,2,0:T(1,128)} %collective-permute-done.1), kind=kLoop, calls=%fused_computation.3 | loop fusion | flops 2527200 | bytes 1591200 | tf_op jit(solution)/shard_map/concatenate | solution.py:35
  93.2 4.1 %all-to-all-done.1 = f32[10,128,1,128]{3,2,0,1:T(1,128)} async-done(((f32[10,128,1,128]{3,2,0,1:T(1,128)}), f32[10,128,1,128]{3,2,0,1:T(1,128)}, u32[]{:S(2)}, u32[]{:S(2)}) %all-to-all-start.1) | async-done | bytes 655392 | tf_op jit(solution)/shard_map/all_to_all | solution.py:107
  97.3 1.1 %copy.240 = f32[10,128,1,128]{3,1,0,2:T(8,128)S(1)} copy(f32[10,128,1,128]{3,2,0,1:T(1,128)} %all-to-all-done.1) | data formatting | bytes 1310720 | tf_op jit(solution)/shard_map/all_to_all | solution.py:107
  98.5 3.8 %fusion.70 = f32[9,8,16,128]{3,1,2,0:T(8,128)S(1)} fusion(f32[10,8,16,1,128]{4,1,2,0,3:T(8,128)S(1)} %bitcast.233, f32[9,8,16,128]{3,1,2,0:T(8,128)S(1)} %copy.134, f32[9,10,16,1]{3,1,2,0:T(8,128)S(1)} %pad.11, f32[9,1,16,128]{3,1,2,0:T(1,128)} %collective-permute-done, f32[9,1,16,128]{3,1,2,0:T(1,128)} %collective-permute-done.1, ...), kind=kLoop, calls=%fused_computation.90 | loop fusion | flops 2949120 | bytes 3239168 | tf_op jit(solution)/shard_map/add | solution.py:120
  (87 shorter events, 15.3 us)
Async XLA Ops:
  0.6 8.6 %copy-start = (f32[9,9]{1,0:T(8,128)S(1)}, f32[9,9]{1,0:T(8,128)}, u32[]{:S(2)}) copy-start(f32[9,9]{1,0:T(8,128)} %param.19) | copy-start | bytes 976
  0.6 9.0 %copy-start.1 = (f32[1,1,32,3,9,128]{5,2,4,3,1,0:T(8,128)S(1)}, f32[1,1,32,3,9,128]{5,2,4,3,1,0:T(8,128)}, u32[]{:S(2)}) copy-start(f32[1,1,32,3,9,128]{5,2,4,3,1,0:T(8,128)} %param.13) | copy-start | bytes 1327108
  0.7 9.0 %copy-start.4 = (s32[1,1,32]{2,1,0:T(1,128)S(1)}, s32[1,1,32]{2,1,0:T(1,128)}, u32[]{:S(2)}) copy-start(s32[1,1,32]{2,1,0:T(1,128)} %param.17) | copy-start | bytes 388
  30.5 3.6 %copy-start.6 = (s32[1,1,32]{2,1,0:T(1,128)S(1)}, s32[1,1,32]{2,1,0:T(1,128)}, u32[]{:S(2)}) copy-start(s32[1,1,32]{2,1,0:T(1,128)} %param.14) | copy-start | bytes 388
  34.0 10.6 %copy-start.2 = (f32[9,8,16,128]{3,2,1,0:T(8,128)S(1)}, f32[9,8,16,128]{3,2,1,0:T(8,128)}, u32[]{:S(2)}) copy-start(f32[9,8,16,128]{3,2,1,0:T(8,128)} %param.12) | copy-start | bytes 1769476
  36.9 22.0 %copy-start.7 = (s32[1,1,32,1]{2,3,1,0:T(1,128)S(1)}, s32[1,1,32,1]{2,3,1,0:T(1,128)}, u32[]{:S(2)}) copy-start(s32[1,1,32,1]{2,3,1,0:T(1,128)} %param.15) | copy-start | bytes 388
  36.9 22.9 %all-to-all-start = ((f32[9,8,16,128]{3,1,0,2:T(8,128)}), f32[9,8,16,128]{3,1,0,2:T(8,128)S(1)}, u32[]{:S(2)}, u32[]{:S(2)}) async-start(f32[9,8,16,128]{3,1,0,2:T(8,128)} %copy.117), calls=%async_computation | async-start | bytes 1179648 | tf_op jit(solution)/shard_map/all_to_all | solution.py:103
  45.3 41.7 %collective-permute-start.2 = (f32[9,8,16,1]{2,1,3,0:T(8,128)S(1)}, f32[9,8,16,1]{2,1,3,0:T(8,128)S(1)}, u32[]{:S(2)}, u32[]{:S(2)}) collective-permute-start(f32[9,8,16,1]{2,1,3,0:T(8,128)S(1)} %copy.163), channel_id=1, source_target_pairs={{0,1},{1,2},{2,3},{3,4},{4,5},{5,6},{6,7},{7,8},{8,9},{9,10},{10,1... | collective-permute-start | bytes 13832 | tf_op jit(solution)/shard_map/ppermute | solution.py:28
  50.2 37.4 %collective-permute-start.3 = (f32[9,8,16,1]{2,1,3,0:T(8,128)S(1)}, f32[9,8,16,1]{2,1,3,0:T(8,128)}, u32[]{:S(2)}, u32[]{:S(2)}) collective-permute-start(f32[9,8,16,1]{2,1,3,0:T(8,128)S(1)} %copy.164), channel_id=1, source_target_pairs={{1,0},{2,1},{3,2},{4,3},{5,4},{6,5},{7,6},{8,7},{9,8},{10,9},{11,1... | collective-permute-start | bytes 13832 | tf_op jit(solution)/shard_map/ppermute | solution.py:29
  52.8 36.3 %collective-permute-start = (f32[9,1,16,128]{3,1,2,0:T(1,128)}, f32[9,1,16,128]{3,1,2,0:T(1,128)}, u32[]{:S(2)}, u32[]{:S(2)}) collective-permute-start(f32[9,1,16,128]{3,1,2,0:T(1,128)} %bitcast.65), channel_id=1, source_target_pairs={{16,0},{32,16},{48,32},{64,48},{80,64},{96,80},{112,96},{128,112},... | collective-permute-start | bytes 221192 | tf_op jit(solution)/shard_map/ppermute | solution.py:29
  54.1 35.0 %collective-permute-start.1 = (f32[9,1,16,128]{3,1,2,0:T(1,128)}, f32[9,1,16,128]{3,1,2,0:T(1,128)}, u32[]{:S(2)}, u32[]{:S(2)}) collective-permute-start(f32[9,1,16,128]{3,1,2,0:T(1,128)} %bitcast.66), channel_id=1, source_target_pairs={{0,16},{16,32},{32,48},{48,64},{64,80},{80,96},{96,112},{112,128},... | collective-permute-start | bytes 221192 | tf_op jit(solution)/shard_map/ppermute | solution.py:28
  59.8 17.3 %all-to-all-start.2 = ((f32[16,1,1]{2,1,0:T(1,128)}), f32[16,1,1]{2,1,0:T(1,128)S(1)}, u32[]{:S(2)}, u32[]{:S(2)}) async-start(f32[16,1,1]{2,1,0:T(1,128)} %copy.135), calls=%async_computation.2 | async-start | bytes 16384 | tf_op jit(solution)/shard_map/all_to_all | solution.py:16
  70.4 15.0 %copy-start.3 = (s32[8,16,1]{1,2,0:T(1,128)S(1)}, s32[8,16,1]{1,2,0:T(1,128)}, u32[]{:S(2)}) copy-start(s32[8,16,1]{1,2,0:T(1,128)} %param.18) | copy-start | bytes 1540
  70.4 15.0 %copy-start.5 = (f32[4]{0:T(128)S(1)}, f32[4]{0:T(128)}, u32[]{:S(2)}) copy-start(f32[4]{0:T(128)} %constant.59.clone) | copy-start | bytes 52
  77.2 20.1 %all-to-all-start.1 = ((f32[10,128,1,128]{3,2,0,1:T(1,128)}), f32[10,128,1,128]{3,2,0,1:T(1,128)}, u32[]{:S(2)}, u32[]{:S(2)}) async-start(f32[10,128,1,128]{3,2,0,1:T(1,128)} %copy.122), calls=%async_computation.1 | async-start | bytes 1310720 | tf_op jit(solution)/shard_map/all_to_all | solution.py:107
where the time goes:
time: 105 us; the launch traced here: 104 us
  starting transfers between devices  38.6 us (37%)
  matrix products  30.9 us (29%)
  local copies, waits for them, and re-layouts  13 us (12%)
  other arithmetic  9.92 us (9%)
  waiting for transfers between devices  8.7 us (8%)
  between operations  3.12 us (3%)
    dot_general x8, matrix products, integrate(): jnp.einsum('km,kmsc->ksc', corrector, history, precision=high)  12.4 us
    dot_general x8, matrix products, integrate(): guess = jnp.einsum('km,kmsc->ksc', predictor, history, precision=high)  12.2 us
    all_to_all x1, starting transfers between devices, sum_at_owner(): lax.all_to_all(pieces, axis, split_axis=0, concat_axis=0, tiled=True)  10.3 us
    ppermute x2, starting transfers between devices, extended(): lax.ppermute(last, axis, up)  9.2 us
    all_to_all x1, starting transfers between devices, shards(): lax.all_to_all(smoothed, 'stream', split_axis=1, concat_axis=2, tiled=True)  8.2 us
    all_to_all x1, starting transfers between devices, shards(): lax.all_to_all(rates, 'stream', split_axis=2, concat_axis=1, tiled=True)  7.7 us
    all_to_all x1, waiting for transfers between devices, sum_at_owner(): lax.all_to_all(pieces, axis, split_axis=0, concat_axis=0, tiled=True)  4.63 us
    concatenate x1, other arithmetic, extended(): jnp.concatenate([jnp.pad(low, around), array, jnp.pad(high, around)], axi...  4.11 us
  transfers between devices with their start and end apart: 7, of which 2 were waited for; matrix products, arithmetic and copies ran while one was open for 12% of the time, Pallas kernels for 0%

commit v1 on v0

v1 whole, which is shorter than its diff:
```python
import functools

import jax
import jax.numpy as jnp
from jax import lax
from jax.experimental import pallas as pl
from jax.experimental.pallas import tpu as pltpu
from jax.sharding import PartitionSpec as P

MESH = pl.DeviceIdType.MESH
F32 = jnp.float32
SUBMAX = 8
NS = 9
SIDE = 4
GROUPS = SIDE * SIDE
CHUNKS = 4
CHUNK_ORDER = (0, 2, 1, 3)


def iota(shape, dim):
    return lax.broadcasted_iota(jnp.int32, shape, dim)


def by_order(order, one, two, three):
    return jnp.where(order == 1, F32(one), jnp.where(order == 2, F32(two), F32(three)))


def column(row, size):
    wide = jnp.broadcast_to(row.astype(F32), (size, size))
    eye = iota((size, size), 0) == iota((size, size), 1)
    return jnp.sum(jnp.where(eye, wide, 0.0), axis=1, keepdims=True)


def kernel(
    spans,
    mech,
    species_hbm,
    history_hbm,
    tiles,
    owners,
    orders,
    steps,
    levels,
    out_hbm,
    load,
    hist,
    sp,
    outv,
    rate,
    sens,
    meta,
    share,
    coef,
    zh,
    yh,
    pack,
    spread,
    wts,
    hist_sem,
    sp_sem,
    out_sem,
    send_sem,
    recv_sem,
    small_send,
    small_recv,
    halo_send,
    halo_recv,
):
    me = lax.axis_index("stream")
    mp = lax.axis_index("span")
    sy, sx = me // SIDE, me % SIDE

    def at(dy, dx):
        return ((sy + dy + SIDE) % SIDE) * SIDE + (sx + dx + SIDE) % SIDE

    barrier = pltpu.get_barrier_semaphore()
    for d in range(1, GROUPS):
        pl.semaphore_signal(barrier, inc=1, device_id={"stream": (me + d) % GROUPS}, device_id_type=MESH)
    for d in range(1, spans):
        pl.semaphore_signal(barrier, inc=1, device_id={"span": (mp + d) % spans}, device_id_type=MESH)

    hist_copy = pltpu.make_async_copy(history_hbm, hist, hist_sem)
    hist_copy.start()
    sp_copy = pltpu.make_async_copy(species_hbm, sp, sp_sem)
    sp_copy.start()

    lane8 = iota((8, 128), 1)
    row8 = iota((8, 128), 0)
    order = jnp.broadcast_to(column(orders[...], 32), (32, 128))
    count = column(steps[...], 32)
    tile = column(tiles[...], 32)
    owner = column(owners[...], 32)
    coef[0] = by_order(order, 1.0, 2.0, 3.0)
    coef[1] = by_order(order, 0.0, -1.0, -3.0)
    coef[2] = by_order(order, 0.0, 0.0, 1.0)
    coef[3] = by_order(order, 1.0, 4.0 / 3.0, 18.0 / 11.0)
    coef[4] = by_order(order, 0.0, -1.0 / 3.0, -9.0 / 11.0)
    coef[5] = by_order(order, 0.0, 0.0, 2.0 / 11.0)
    coef[6] = by_order(order, 0.5, 0.5 * 2.0 / 3.0, 0.5 * 6.0 / 11.0)
    count_b = jnp.broadcast_to(count, (32, 128))
    coef[7] = count_b
    coef[8] = 1.0 / jnp.maximum(count_b, 1.0)

    tile_z = jnp.floor(tile * (1.0 / 16.0))
    tile_x = jnp.broadcast_to(tile - 16.0 * tile_z, (32, 128))
    tile_z = jnp.broadcast_to(tile_z + 8.0 * me.astype(F32), (32, 128))
    mine = (lane8 // 8 == me) & (lane8 % 8 == row8)
    table = jnp.zeros((8, 128), F32)
    for c in range(CHUNKS):
        for k, values in ((0, tile_z), (4, tile_x)):
            line = jnp.sum(jnp.where(mine, values[8 * c : 8 * c + 8], 0.0), axis=0, keepdims=True)
            table = jnp.where(row8 == c + k, jnp.broadcast_to(line, (8, 128)), table)
    meta[me] = table
    lane32 = iota((32, 128), 1).astype(F32)
    owed = jnp.sum(jnp.where(owner == lane32, count_b, 0.0), axis=0, keepdims=True)
    share[mp] = owed

    def send_chunk(c, src, dst):
        pltpu.make_async_remote_copy(
            src_ref=rate.at[c, src],
            dst_ref=rate.at[c, src],
            send_sem=send_sem,
            recv_sem=recv_sem.at[c, src],
            device_id={"stream": dst},
            device_id_type=MESH,
        ).start()

    def directions(c):
        return c < 2, 1 if c % 2 == 0 else -1

    def step_to(c, first, second):
        x_first, _ = directions(c)
        return at(second, first) if x_first else at(first, second)

    def forward(c, src, df, dg):
        _, e = directions(c)
        if dg == 0:
            if df == 0:
                send_chunk(c, src, step_to(c, e, 0))
                send_chunk(c, src, step_to(c, -e, 0))
            elif df == e:
                send_chunk(c, src, step_to(c, e, 0))
            send_chunk(c, src, step_to(c, 0, e))
            send_chunk(c, src, step_to(c, 0, -e))
        elif dg == e:
            send_chunk(c, src, step_to(c, 0, e))

    def arrive(c, df, dg):
        src = step_to(c, -df, -dg)
        pltpu.make_async_copy(rate.at[c, src], rate.at[c, src], recv_sem.at[c, src]).wait()
        forward(c, src, df, dg)

    hist_copy.wait()

    def chemistry(c):
        rows = slice(8 * c, 8 * c + 8)
        p1, p2, p3, a1, a2, a3, hb, cnt, inv = [coef[k, rows, :] for k in range(9)]
        h1, h2, h3 = [tuple(hist[m, s, rows, :] for s in range(NS)) for m in range(3)]

        def substep(n, carry):
            h1, h2, h3, last = carry
            guess = [p1 * h1[s] + p2 * h2[s] + p3 * h3[s] for s in range(NS)]
            active = cnt > n.astype(F32)
            fresh = []
            done = []
            for s in range(NS):
                total = mech[s, 0] * guess[0]
                for t in range(1, NS):
                    total = total + mech[s, t] * guess[t]
                y = a1 * h1[s] + a2 * h2[s] + a3 * h3[s] + hb * jnp.tanh(total)
                fresh.append(y)
                done.append(jnp.where(active, y, last[s]))
            return tuple(fresh), h1, h2, tuple(done)

        _, _, _, last = lax.fori_loop(0, SUBMAX, substep, (h1, h2, h3, h1))
        for s in range(NS):
            rate[c, me, s] = (last[s] - hist[0, s, rows, :]) * inv

    chemistry(CHUNK_ORDER[0])
    pl.semaphore_wait(barrier, (GROUPS - 1) + (spans - 1))
    forward(CHUNK_ORDER[0], me, 0, 0)
    for d in range(1, GROUPS):
        pltpu.make_async_remote_copy(
            meta.at[me], meta.at[me], small_send.at[0], small_recv.at[0], device_id={"stream": (me + d) % GROUPS}, device_id_type=MESH
        ).start()
    for d in range(1, spans):
        pltpu.make_async_remote_copy(
            share.at[mp], share.at[mp], small_send.at[1], small_recv.at[1], device_id={"span": (mp + d) % spans}, device_id_type=MESH
        ).start()
    for c in CHUNK_ORDER[1:]:
        chemistry(c)
        forward(c, me, 0, 0)

    sp_copy.wait()
    halo = [
        pltpu.make_async_remote_copy(
            sp.at[:, 7], zh.at[0], halo_send.at[0], halo_recv.at[0], device_id={"stream": (me + 1) % GROUPS}, device_id_type=MESH
        ),
        pltpu.make_async_remote_copy(
            sp.at[:, 0], zh.at[1], halo_send.at[1], halo_recv.at[1], device_id={"stream": (me + GROUPS - 1) % GROUPS}, device_id_type=MESH
        ),
    ]
    for copy in halo:
        copy.start()
    lane = iota((8, 16, 128), 2)
    packed = jnp.zeros((8, 16, 128), F32)
    for s in range(NS):
        turned = pltpu.roll(sp[s], 2 * s + 2, 2)
        packed = jnp.where((lane == 2 * s + 1) | (lane == 2 * s + 2), turned, packed)
    pack[...] = packed
    for k, dst in ((2, (mp + 1) % spans), (3, (mp + spans - 1) % spans)):
        copy = pltpu.make_async_remote_copy(
            pack, yh.at[k - 2], halo_send.at[k], halo_recv.at[k], device_id={"span": dst}, device_id_type=MESH
        )
        copy.start()
        halo.append(copy)

    def level(n):
        for c in CHUNK_ORDER:
            _, e = directions(c)
            hops = {0: 0, e: 1, -e: 1, 2 * e: 2}
            for df in hops:
                for dg in hops:
                    if hops[df] + hops[dg] == n:
                        arrive(c, df, dg)

    level(1)

    for copy in halo:
        copy.wait()
    below = jnp.where(me > 0, 1.0, 0.0).astype(F32)
    above = jnp.where(me < GROUPS - 1, 1.0, 0.0).astype(F32)
    left = jnp.where(mp > 0, 1.0, 0.0).astype(F32)
    right = jnp.where(mp < spans - 1, 1.0, 0.0).astype(F32)
    xs = iota((8, 16, 128), 1)
    edge = jnp.where(lane % 2 == 0, pltpu.roll(yh[1], 126, 2) * right, yh[0] * left)
    for s in range(NS):
        cells = sp[s]
        ends = pltpu.roll(edge, 127 - 2 * s, 2)
        zdown = jnp.concatenate([(zh[0, s] * below)[None], cells[:-1]], axis=0)
        zup = jnp.concatenate([cells[1:], (zh[1, s] * above)[None]], axis=0)
        xdown = jnp.where(xs == 0, 0.0, pltpu.roll(cells, 1, 1))
        xup = jnp.where(xs == 15, 0.0, pltpu.roll(cells, 15, 1))
        ydown = jnp.where(lane == 0, ends, pltpu.roll(cells, 1, 2))
        yup = jnp.where(lane == 127, ends, pltpu.roll(cells, 127, 2))
        spread[s] = zup + zdown + xup + xdown + yup + ydown - 6.0 * cells

    level(2)

    pltpu.make_async_copy(share.at[pl.ds(0, spans - 1)], share.at[pl.ds(0, spans - 1)], small_recv.at[1]).wait()
    owed = share[0]
    for g in range(1, spans):
        owed = owed + share[g]
    here = jnp.where(iota((1, 128), 1) == mp, owed, 0.0)
    load[...] = jnp.sum(here, axis=1, keepdims=True).astype(jnp.int32)

    pltpu.make_async_copy(meta.at[pl.ds(0, GROUPS - 1)], meta.at[pl.ds(0, GROUPS - 1)], small_recv.at[0]).wait()
    table = meta[0]
    for g in range(1, GROUPS):
        table = table + meta[g]
    cell = iota((128, 128), 0)
    cell_z = (8 * me + cell // 16).astype(F32)
    cell_x = (cell % 16).astype(F32)

    def gauss(other):
        offset = (cell_z - other) * (1.0 / 16.0)
        return jnp.exp(-0.5 * offset * offset)

    norm = 1.0 / jnp.sum(gauss(iota((128, 128), 1).astype(F32)), axis=1, keepdims=True)
    for c in range(CHUNKS):
        wts[c] = jnp.where(cell_x == table[c + 4 : c + 5], gauss(table[c : c + 1]) * norm, 0.0)

    level(3)
    level(4)

    for c in range(CHUNKS):
        power = jnp.zeros((GROUPS, 8, 128), F32)
        for s in range(NS):
            power = power + rate[c, :, s] * rate[c, :, s]
        power = power * (1.0 / NS)
        sens[c] = power / (power + 1.0)

    def filtered(parts):
        total = jnp.zeros((128, 128), F32)
        for c in range(CHUNKS):
            total = total + jnp.dot(
                wts[c], parts(c).reshape(128, 128), precision=lax.Precision.HIGHEST, preferred_element_type=F32
            )
        return total

    peaks = []
    for z in range(8):
        wide = jnp.broadcast_to(levels[z], (16, 16))
        eye = iota((16, 16), 0) == iota((16, 16), 1)
        kind = jnp.sum(jnp.where(eye, wide.astype(F32), 0.0), axis=1, keepdims=True)
        peaks.append(jnp.where(kind == 0, 1.5, jnp.where(kind == 1, 4.0, jnp.where(kind == 2, 9.0, 19.0))))
    peak = jnp.concatenate(peaks, axis=0).astype(F32)
    thick = 1.0 + peak * filtered(lambda c: sens[c])
    stretch = 0.02 * thick
    damp = 4.0 / thick
    outs = []
    for s in range(NS):
        fine = filtered(lambda c: rate[c, :, s])
        value = sp[s].reshape(128, 128) + stretch * spread[s].reshape(128, 128) + fine * damp
        outv[s] = value.reshape(8, 16, 128)
        copy = pltpu.make_async_copy(outv.at[s], out_hbm.at[s], out_sem.at[s])
        copy.start()
        outs.append(copy)
    for copy in outs:
        copy.wait()
    for c in range(CHUNKS):
        sent = rate.at[c, pl.ds(0, GROUPS - 1)]
        pltpu.make_async_copy(sent, sent, send_sem).wait()
    pltpu.make_async_copy(meta.at[pl.ds(0, GROUPS - 1)], meta.at[pl.ds(0, GROUPS - 1)], small_send.at[0]).wait()
    pltpu.make_async_copy(share.at[pl.ds(0, spans - 1)], share.at[pl.ds(0, spans - 1)], small_send.at[1]).wait()


def shards(spans, species, history, flame_tiles, owners, orders, substeps, levels, mechanism):
    states = jnp.transpose(history, (0, 1, 3, 4, 2, 5)).reshape(3, NS, 32, 128)
    vmem = pl.BlockSpec(memory_space=pltpu.VMEM)
    anywhere = pl.BlockSpec(memory_space=pl.ANY)
    out, load = pl.pallas_call(
        functools.partial(kernel, spans),
        out_shape=(
            jax.ShapeDtypeStruct(species.shape, F32),
            jax.ShapeDtypeStruct((1, 1), jnp.int32),
        ),
        in_specs=[pl.BlockSpec(memory_space=pltpu.SMEM), anywhere, anywhere] + [vmem] * 5,
        out_specs=(anywhere, vmem),
        scratch_shapes=[
            pltpu.VMEM((3, NS, 32, 128), F32),
            pltpu.VMEM((NS, 8, 16, 128), F32),
            pltpu.VMEM((NS, 8, 16, 128), F32),
            pltpu.VMEM((CHUNKS, GROUPS, NS, 8, 128), F32),
            pltpu.VMEM((CHUNKS, GROUPS, 8, 128), F32),
            pltpu.VMEM((GROUPS, 8, 128), F32),
            pltpu.VMEM((spans, 1, 128), F32),
            pltpu.VMEM((9, 32, 128), F32),
            pltpu.VMEM((2, NS, 16, 128), F32),
            pltpu.VMEM((2, 8, 16, 128), F32),
            pltpu.VMEM((8, 16, 128), F32),
            pltpu.VMEM((NS, 8, 16, 128), F32),
            pltpu.VMEM((CHUNKS, 128, 128), F32),
            pltpu.SemaphoreType.DMA,
            pltpu.SemaphoreType.DMA,
            pltpu.SemaphoreType.DMA((NS,)),
            pltpu.SemaphoreType.DMA,
            pltpu.SemaphoreType.DMA((CHUNKS, GROUPS)),
            pltpu.SemaphoreType.DMA((2,)),
            pltpu.SemaphoreType.DMA((2,)),
            pltpu.SemaphoreType.DMA((4,)),
            pltpu.SemaphoreType.DMA((4,)),
        ],
        compiler_params=pltpu.CompilerParams(collective_id=0, has_side_effects=True),
    )(
        mechanism,
        species,
        states,
        flame_tiles.reshape(1, 32),
        owners.reshape(1, 32),
        orders.reshape(1, 32),
        substeps.reshape(1, 32),
        jnp.transpose(levels, (0, 2, 1)),
    )
    return out, load


def solution(mesh):
    in_specs = (
        P(None, "stream", None, "span"),
        P("stream", "span", None, None, None, None),
        P("stream", "span", None),
        P("stream", "span", None, None),
        P("stream", "span", None),
        P("stream", "span", None),
        P("stream", None, "span"),
        P(),
    )
    out_specs = (P(None, "stream", None, "span"), P("stream", "span"))
    return jax.shard_map(
        functools.partial(shards, mesh.shape["span"]),
        mesh=mesh,
        in_specs=in_specs,
        out_specs=out_specs,
        check_vma=False,
    )
```

time: 105 us -> 39.3 us (0.37)
  the two profiles are of different devices: /device:TPU:1 before, /device:TPU:4 now
where the time goes in v1:
time: 39.3 us; the launch traced here: 39.1 us
  Pallas kernels  34.7 us (88%)
  between operations  2.44 us (6%)
  local copies, waits for them, and re-layouts  1.92 us (5%)
    pallas_call x1, Pallas kernels, shards(): pl.pallas_call(functools.partial(kernel, spans), out_shape=(jax.ShapeDtyp...  34.7 us
    unnamed x1, local copies, waits for them, and re-layouts  1.92 us

profile of v1, /device:TPU:4, one launch (start us, length us, event | category | flops | bytes accessed | tf_op | source)
XLA Modules:
  0.0 39.1 jit_solution(9876691136050171968)
XLA Ops:
  0.6 34.7 %shard_map.95 = (f32[9,8,16,128]{3,2,1,0:T(8,128)}, s32[1,1]{1,0:T(1,128)}) custom-call(f32[9,9]{1,0:T(8,128)} %mech.1, f32[9,8,16,128]{3,2,1,0:T(8,128)} %species_hbm.1, f32[3,9,32,128]{3,2,1,0:T(8,128)} %bitcast.10, s32[1,32]{1,0:T(1,128)} %bitcast.12, s32[1,32]{1,0:T(1,128)} %bitcast.13, s32[1,32]{1,0:T(1,128)} %bitcast.14, s32[1,32]{1,0:T(1,128)} %bitcast.15, ...), custom_call_target="tpu_custom_call" | custom-call | tf_op jit(solution)/shard_map/pallas_call | solution.py:322
  35.4 1.9 %copy.13 = f32[9,8,16,128]{3,2,1,0:T(8,128)} copy(f32[9,8,16,128]{3,2,1,0:T(8,128)} %get-tuple-element.4) | data formatting | bytes 1179648

commit v2 on v1

v2 whole, which is shorter than its diff:
```python
import functools

import jax
import jax.numpy as jnp
from jax import lax
from jax.experimental import pallas as pl
from jax.experimental.pallas import tpu as pltpu
from jax.sharding import PartitionSpec as P

MESH = pl.DeviceIdType.MESH
F32 = jnp.float32
BF16 = jnp.bfloat16
SUBMAX = 8
NS = 9
SIDE = 4
GROUPS = SIDE * SIDE
CHUNKS = 4
ROWS = 8 * NS + 1
ORDER = (0, 2, 1, 3)


def iota(shape, dim):
    return lax.broadcasted_iota(jnp.int32, shape, dim)


def by_order(order, one, two, three):
    return jnp.where(order == 1, F32(one), jnp.where(order == 2, F32(two), F32(three)))


def column(row, size):
    wide = jnp.broadcast_to(row.astype(F32), (size, size))
    eye = iota((size, size), 0) == iota((size, size), 1)
    return jnp.sum(jnp.where(eye, wide, 0.0), axis=1, keepdims=True)


def sign(c):
    return 1 if c % 2 == 0 else -1


def arrivals():
    found = []
    for n in range(5):
        for c in ORDER:
            e = sign(c)
            hops = {0: 0, e: 1, -e: 1, 2 * e: 2}
            found += [(c, df, dg) for df in hops for dg in hops if hops[df] + hops[dg] == n]
    return found


def kernel(
    spans,
    mech,
    species_hbm,
    history_hbm,
    tiles,
    owners,
    orders,
    steps,
    levels,
    out,
    load_out,
    load,
    hist,
    sp,
    rate,
    share,
    coef,
    zh,
    yh,
    pack,
    spread,
    acc,
    hist_sem,
    sp_sem,
    send_sem,
    recv_sem,
    share_send,
    share_recv,
    halo_send,
    halo_recv,
):
    me = lax.axis_index("stream")
    mp = lax.axis_index("span")
    sy, sx = me // SIDE, me % SIDE

    hist_copy = pltpu.make_async_copy(history_hbm, hist, hist_sem)
    hist_copy.start()
    sp_copy = pltpu.make_async_copy(species_hbm, sp, sp_sem)
    sp_copy.start()

    def at(dy, dx):
        return ((sy + dy + SIDE) % SIDE) * SIDE + (sx + dx + SIDE) % SIDE

    after, before = (me + 1) % GROUPS, (me + GROUPS - 1) % GROUPS
    barrier = pltpu.get_barrier_semaphore()
    for peer in (at(0, 1), at(0, -1), at(1, 0), at(-1, 0), after, before):
        pl.semaphore_signal(barrier, inc=1, device_id={"stream": peer}, device_id_type=MESH)
    for d in range(1, spans):

        @pl.when(mp + d < spans)
        def _():
            pl.semaphore_signal(barrier, inc=1, device_id={"span": mp + d}, device_id_type=MESH)

    order = jnp.broadcast_to(column(orders[...], 32), (32, 128))
    count = column(steps[...], 32)
    tile = column(tiles[...], 32)
    owner = column(owners[...], 32)
    coef[0] = by_order(order, 1.0, 2.0, 3.0)
    coef[1] = by_order(order, 0.0, -1.0, -3.0)
    coef[2] = by_order(order, 0.0, 0.0, 1.0)
    coef[3] = by_order(order, 1.0, 4.0 / 3.0, 18.0 / 11.0)
    coef[4] = by_order(order, 0.0, -1.0 / 3.0, -9.0 / 11.0)
    coef[5] = by_order(order, 0.0, 0.0, 2.0 / 11.0)
    coef[6] = by_order(order, 0.5, 0.5 * 2.0 / 3.0, 0.5 * 6.0 / 11.0)
    count_b = jnp.broadcast_to(count, (32, 128))
    coef[7] = count_b
    coef[8] = 1.0 / jnp.maximum(count_b, 1.0)

    cell_of = jnp.broadcast_to(tile + (128 * me).astype(F32), (32, 128))
    mine = iota((8, 128), 1) % 8 == iota((8, 128), 0)
    for c in range(CHUNKS):
        rate[c, me, 8 * NS : ROWS, :] = jnp.sum(jnp.where(mine, cell_of[8 * c : 8 * c + 8], 0.0), axis=0, keepdims=True)
    lane32 = iota((32, 128), 1).astype(F32)
    share[mp] = jnp.sum(jnp.where(owner == lane32, count_b, 0.0), axis=0, keepdims=True)

    def send_chunk(c, src, dst):
        pltpu.make_async_remote_copy(
            src_ref=rate.at[c, src],
            dst_ref=rate.at[c, src],
            send_sem=send_sem,
            recv_sem=recv_sem.at[c, src],
            device_id={"stream": dst},
            device_id_type=MESH,
        ).start()

    def step_to(c, first, second):
        return at(second, first) if c < 2 else at(first, second)

    def forward(c, df, dg):
        src = step_to(c, -df, -dg)
        e = sign(c)
        if dg == 0:
            if df == 0:
                send_chunk(c, src, step_to(c, e, 0))
                send_chunk(c, src, step_to(c, -e, 0))
            elif df == e:
                send_chunk(c, src, step_to(c, e, 0))
            send_chunk(c, src, step_to(c, 0, e))
            send_chunk(c, src, step_to(c, 0, -e))
        elif dg == e:
            send_chunk(c, src, step_to(c, 0, e))

    def arrive(c, df, dg):
        if (df, dg) != (0, 0):
            src = step_to(c, -df, -dg)
            pltpu.make_async_copy(rate.at[c, src], rate.at[c, src], recv_sem.at[c, src]).wait()
            forward(c, df, dg)

    def chemistry(c):
        rows = slice(8 * c, 8 * c + 8)
        p1, p2, p3, a1, a2, a3, hb, cnt, inv = [coef[k, rows, :] for k in range(9)]
        h1, h2, h3 = [tuple(hist[m, s, rows, :] for s in range(NS)) for m in range(3)]

        def substep(n, carry):
            h1, h2, h3, last = carry
            guess = [p1 * h1[s] + p2 * h2[s] + p3 * h3[s] for s in range(NS)]
            active = cnt > n.astype(F32)
            fresh = []
            done = []
            for s in range(NS):
                total = mech[s, 0] * guess[0]
                for t in range(1, NS):
                    total = total + mech[s, t] * guess[t]
                y = a1 * h1[s] + a2 * h2[s] + a3 * h3[s] + hb * jnp.tanh(total)
                fresh.append(y)
                done.append(jnp.where(active, y, last[s]))
            return tuple(fresh), h1, h2, tuple(done)

        _, _, _, last = lax.fori_loop(0, SUBMAX, substep, (h1, h2, h3, h1))
        for s in range(NS):
            rate[c, me, 8 * s : 8 * s + 8, :] = (last[s] - hist[0, s, rows, :]) * inv

    hist_copy.wait()
    chemistry(ORDER[0])
    sp_copy.wait()
    lane = iota((8, 16, 128), 2)
    packed = jnp.zeros((8, 16, 128), F32)
    for s in range(NS):
        turned = pltpu.roll(sp[s], 2 * s + 2, 2)
        packed = jnp.where((lane == 2 * s + 1) | (lane == 2 * s + 2), turned, packed)
    pack[...] = packed
    chemistry(ORDER[1])
    chemistry(ORDER[2])
    pl.semaphore_wait(barrier, 6 + mp)
    for c in ORDER[:3]:
        forward(c, 0, 0)
    chemistry(ORDER[3])
    forward(ORDER[3], 0, 0)

    z_halo = [
        pltpu.make_async_remote_copy(
            sp.at[:, 7], zh.at[0], halo_send.at[0], halo_recv.at[0], device_id={"stream": after}, device_id_type=MESH
        ),
        pltpu.make_async_remote_copy(
            sp.at[:, 0], zh.at[1], halo_send.at[1], halo_recv.at[1], device_id={"stream": before}, device_id_type=MESH
        ),
    ]
    for copy in z_halo:
        copy.start()

    def send_share(dst):
        pltpu.make_async_remote_copy(
            share.at[mp], share.at[mp], share_send.at[dst], share_recv.at[mp], device_id={"span": dst}, device_id_type=MESH
        ).start()

    def wait_share(sem, k):
        pltpu.make_async_copy(share.at[k], share.at[k], sem.at[k]).wait()

    def halo_copy(slot, dst):
        return pltpu.make_async_remote_copy(
            pack, yh.at[slot], halo_send.at[2 + slot], halo_recv.at[2 + slot], device_id={"span": dst}, device_id_type=MESH
        )

    def wait_halo(sem, slot):
        pltpu.make_async_copy(yh.at[slot], yh.at[slot], sem.at[2 + slot]).wait()

    @pl.when(mp > 0)
    def _():
        halo_copy(1, mp - 1).start()

    for d in range(1, spans):

        @pl.when(mp >= d)
        def _():
            send_share(mp - d)

    cell = iota((128, 128), 0) + 128 * me
    cell_z = (cell // 16).astype(F32)
    cell_x = (cell % 16).astype(F32)
    lane2 = iota((1, 128), 1)

    def gauss(other):
        offset = (cell_z - other) * (1.0 / 16.0)
        return jnp.exp(-0.5 * offset * offset)

    norm = 1.0 / jnp.sum(gauss(iota((128, 128), 1).astype(F32)), axis=1, keepdims=True)

    def filter_part(slots, initial):
        refs = [(c, step_to(c, -df, -dg)) for c, df, dg in slots]
        cells = jnp.zeros((1, 128), F32)
        for k, (c, src) in enumerate(refs):
            cells = jnp.where(lane2 // 8 == k, rate[c, src, 8 * NS : ROWS, :], cells)
        z = jnp.floor(cells * (1.0 / 16.0))
        x = cells - 16.0 * z
        weight = jnp.where(cell_x == x, gauss(z) * norm, 0.0)
        high = weight.astype(BF16)
        low = (weight - high.astype(F32)).astype(BF16)
        left = jnp.concatenate([high, high, low], axis=1)

        def split(values):
            high = values.astype(BF16)
            low = (values - high.astype(F32)).astype(BF16)
            return jnp.concatenate([high, low, high], axis=0)

        values = [jnp.concatenate([rate[c, src, 8 * s : 8 * s + 8, :] for c, src in refs], axis=0) for s in range(NS)]
        power = values[0] * values[0]
        for s in range(1, NS):
            power = power + values[s] * values[s]
        power = power * (1.0 / NS)
        values = [power / (power + 1.0)] + values
        for k in range(5):
            right = jnp.concatenate([split(values[2 * k]), split(values[2 * k + 1])], axis=1)
            part = jnp.dot(left, right, preferred_element_type=F32)
            if not initial:
                part = part + acc[k]
            acc[k] = part

    events = arrivals()
    for event in events[:16]:
        arrive(*event)
    filter_part(events[:16], True)
    for event in events[16:32]:
        arrive(*event)
    filter_part(events[16:32], False)

    @pl.when(mp < spans - 1)
    def _():
        wait_halo(halo_recv, 1)
        halo_copy(0, mp + 1).start()

    for d in range(1, spans):

        @pl.when(mp + d < spans)
        def _():
            wait_share(share_recv, mp + d)
            send_share(mp + d)

    for event in events[32:48]:
        arrive(*event)
    filter_part(events[32:48], False)

    for copy in z_halo:
        copy.wait()

    @pl.when(mp > 0)
    def _():
        wait_halo(halo_recv, 0)
        wait_halo(halo_send, 1)

    @pl.when(mp < spans - 1)
    def _():
        wait_halo(halo_send, 0)

    @pl.when(mp == 0)
    def _():
        yh[0] = jnp.zeros((8, 16, 128), F32)

    @pl.when(mp == spans - 1)
    def _():
        yh[1] = jnp.zeros((8, 16, 128), F32)

    below, above = me > 0, me < GROUPS - 1
    xs = iota((8, 16, 128), 1)
    edge = jnp.where(lane % 2 == 0, pltpu.roll(yh[1], 126, 2), yh[0])
    for s in range(NS):
        cells = sp[s]
        ends = pltpu.roll(edge, 127 - 2 * s, 2)
        zdown = jnp.concatenate([jnp.where(below, zh[0, s], 0.0)[None], cells[:-1]], axis=0)
        zup = jnp.concatenate([cells[1:], jnp.where(above, zh[1, s], 0.0)[None]], axis=0)
        xdown = jnp.where(xs == 0, 0.0, pltpu.roll(cells, 1, 1))
        xup = jnp.where(xs == 15, 0.0, pltpu.roll(cells, 15, 1))
        ydown = jnp.where(lane == 0, ends, pltpu.roll(cells, 1, 2))
        yup = jnp.where(lane == 127, ends, pltpu.roll(cells, 127, 2))
        spread[s] = zup + zdown + xup + xdown + yup + ydown - 6.0 * cells

    for d in range(1, spans):

        @pl.when(mp >= d)
        def _():
            wait_share(share_recv, mp - d)
            wait_share(share_send, mp - d)

        @pl.when(mp + d < spans)
        def _():
            wait_share(share_send, mp + d)

    owed = share[0]
    for g in range(1, spans):
        owed = owed + share[g]
    here = jnp.where(lane2 == mp, owed, 0.0)
    load[...] = jnp.sum(here, axis=1, keepdims=True).astype(jnp.int32)
    load_copy = pltpu.make_async_copy(load, load_out, hist_sem)
    load_copy.start()

    peaks = []
    for z in range(8):
        wide = jnp.broadcast_to(levels[z], (16, 16))
        eye = iota((16, 16), 0) == iota((16, 16), 1)
        kind = jnp.sum(jnp.where(eye, wide.astype(F32), 0.0), axis=1, keepdims=True)
        peaks.append(jnp.where(kind == 0, 1.5, jnp.where(kind == 1, 4.0, jnp.where(kind == 2, 9.0, 19.0))))
    peak = jnp.concatenate(peaks, axis=0).astype(F32)

    for event in events[48:]:
        arrive(*event)
    filter_part(events[48:], False)

    thick = 1.0 + peak * acc[0, :, 0:128]
    stretch = 0.02 * thick
    damp = 4.0 / thick
    for s in range(NS):
        k, half = (s + 1) // 2, (s + 1) % 2
        fine = acc[k, :, 128 * half : 128 * half + 128]
        value = sp[s].reshape(128, 128) + stretch * spread[s].reshape(128, 128) + fine * damp
        out[s] = value.reshape(8, 16, 128)
    load_copy.wait()
    for c in range(CHUNKS):
        sent = rate.at[c, pl.ds(0, GROUPS - 1)]
        pltpu.make_async_copy(sent, sent, send_sem).wait()


def deliver(out, load, out_hbm, load_hbm, sems):
    copies = [
        pltpu.make_async_copy(out, out_hbm, sems.at[0]),
        pltpu.make_async_copy(load, load_hbm, sems.at[1]),
    ]
    for copy in copies:
        copy.start()
    for copy in copies:
        copy.wait()


def shards(spans, species, history, flame_tiles, owners, orders, substeps, levels, mechanism):
    states = jnp.transpose(history, (0, 1, 3, 4, 2, 5)).reshape(3, NS, 32, 128)
    vmem = pl.BlockSpec(memory_space=pltpu.VMEM)
    anywhere = pl.BlockSpec(memory_space=pl.ANY)
    results = (
        jax.ShapeDtypeStruct(species.shape, F32),
        jax.ShapeDtypeStruct((1, 1), jnp.int32),
    )
    out, load = pl.pallas_call(
        functools.partial(kernel, spans),
        out_shape=(pltpu.VMEM(species.shape, F32), results[1]),
        in_specs=[pl.BlockSpec(memory_space=pltpu.SMEM), anywhere, anywhere] + [vmem] * 5,
        out_specs=(vmem, anywhere),
        scratch_shapes=[
            pltpu.VMEM((1, 1), jnp.int32),
            pltpu.VMEM((3, NS, 32, 128), F32),
            pltpu.VMEM((NS, 8, 16, 128), F32),
            pltpu.VMEM((CHUNKS, GROUPS, ROWS, 128), F32),
            pltpu.VMEM((spans, 1, 128), F32),
            pltpu.VMEM((9, 32, 128), F32),
            pltpu.VMEM((2, NS, 16, 128), F32),
            pltpu.VMEM((2, 8, 16, 128), F32),
            pltpu.VMEM((8, 16, 128), F32),
            pltpu.VMEM((NS, 8, 16, 128), F32),
            pltpu.VMEM((5, 128, 256), F32),
            pltpu.SemaphoreType.DMA,
            pltpu.SemaphoreType.DMA,
            pltpu.SemaphoreType.DMA,
            pltpu.SemaphoreType.DMA((CHUNKS, GROUPS)),
            pltpu.SemaphoreType.DMA((spans,)),
            pltpu.SemaphoreType.DMA((spans,)),
            pltpu.SemaphoreType.DMA((4,)),
            pltpu.SemaphoreType.DMA((4,)),
        ],
        compiler_params=pltpu.CompilerParams(
            collective_id=0, has_side_effects=True
        ),
    )(
        mechanism,
        species,
        states,
        flame_tiles.reshape(1, 32),
        owners.reshape(1, 32),
        orders.reshape(1, 32),
        substeps.reshape(1, 32),
        jnp.transpose(levels, (0, 2, 1)),
    )
    return pl.pallas_call(
        deliver,
        out_shape=results,
        in_specs=[anywhere, anywhere],
        out_specs=(anywhere, anywhere),
        scratch_shapes=[pltpu.SemaphoreType.DMA((2,))],
        compiler_params=pltpu.CompilerParams(vmem_limit_bytes=2**20),
    )(out, load)


def solution(mesh):
    in_specs = (
        P(None, "stream", None, "span"),
        P("stream", "span", None, None, None, None),
        P("stream", "span", None),
        P("stream", "span", None, None),
        P("stream", "span", None),
        P("stream", "span", None),
        P("stream", None, "span"),
        P(),
    )
    out_specs = (P(None, "stream", None, "span"), P("stream", "span"))
    return jax.shard_map(
        functools.partial(shards, mesh.shape["span"]),
        mesh=mesh,
        in_specs=in_specs,
        out_specs=out_specs,
        check_vma=False,
    )
```

time: 39.3 us -> 28.6 us (0.73)
  Pallas kernels: 34.7 us -> 27.8 us
  local copies, waits for them, and re-layouts: 1.92 us -> 0 us
  between operations: 2.44 us -> 0.64 us
    pallas_call x1 -> x2, Pallas kernels: 34.7 us -> 27.8 us  [the longest x1 26.4 us: shards(): pl.pallas_call(functools.partial(kernel, spans), out_shape=(pltpu.VMEM(sp...]
    unnamed x1 -> x0, local copies, waits for them, and re-layouts: 1.92 us -> none
where the time goes in v2:
time: 28.6 us; the launch traced here: 28.4 us
  Pallas kernels  27.8 us (97%)
  between operations  0.64 us (2%)
    pallas_call x1, Pallas kernels, shards(): pl.pallas_call(functools.partial(kernel, spans), out_shape=(pltpu.VMEM(sp...  26.4 us
    pallas_call x1, Pallas kernels, shards(): pl.pallas_call(deliver, out_shape=results, in_specs=[anywhere, anywhere],...  1.39 us

profile of v2, /device:TPU:4, one launch (start us, length us, event | category | flops | bytes accessed | tf_op | source)
XLA Modules:
  0.0 28.4 jit_solution(813723890583112953)
XLA Ops:
  0.6 26.4 %shard_map.95 = (f32[9,8,16,128]{3,2,1,0:T(8,128)S(1)}, s32[1,1]{1,0:T(1,128)}) custom-call(f32[9,9]{1,0:T(8,128)} %mech.1, f32[9,8,16,128]{3,2,1,0:T(8,128)} %species_hbm.1, f32[3,9,32,128]{3,2,1,0:T(8,128)} %bitcast.10, s32[1,32]{1,0:T(1,128)} %bitcast.12, s32[1,32]{1,0:T(1,128)} %bitcast.13, s32[1,32]{1,0:T(1,128)} %bitcast.14, s32[1,32]{1,0:T(1,128)} %bitcast.15, ...), custom_call_target="tpu_custom_call" | custom-call | tf_op jit(solution)/shard_map/pallas_call | solution.py:400
  27.0 1.4 %shard_map.96 = (f32[9,8,16,128]{3,2,1,0:T(8,128)}, s32[1,1]{1,0:T(1,128)}) custom-call(f32[9,8,16,128]{3,2,1,0:T(8,128)S(1)} %get-tuple-element.4.out, s32[1,1]{1,0:T(1,128)} %get-tuple-element.5.load), custom_call_target="tpu_custom_call" | custom-call | tf_op jit(solution)/shard_map/pallas_call | solution.py:439

commit v3 on v2

--- a/solution.py
+++ b/solution.py
@@ -15,8 +15,10 @@
 SIDE = 4
 GROUPS = SIDE * SIDE
 CHUNKS = 4
-ROWS = 8 * NS + 1
-ORDER = (0, 2, 1, 3)
+STEPS = (
+    (2, 2), (1, 2), (2, 1), (3, 2), (2, 3), (1, 1), (3, 3), (1, 3),
+    (3, 1), (0, 2), (2, 0), (0, 1), (1, 0), (0, 3), (3, 0), (0, 0),
+)
 
 
 def iota(shape, dim):
@@ -31,20 +33,6 @@
     wide = jnp.broadcast_to(row.astype(F32), (size, size))
     eye = iota((size, size), 0) == iota((size, size), 1)
     return jnp.sum(jnp.where(eye, wide, 0.0), axis=1, keepdims=True)
-
-
-def sign(c):
-    return 1 if c % 2 == 0 else -1
-
-
-def arrivals():
-    found = []
-    for n in range(5):
-        for c in ORDER:
-            e = sign(c)
-            hops = {0: 0, e: 1, -e: 1, 2 * e: 2}
-            found += [(c, df, dg) for df in hops for dg in hops if hops[df] + hops[dg] == n]
-    return found
 
 
 def kernel(
@@ -63,17 +51,22 @@
     hist,
     sp,
     rate,
+    go_out,
+    go_in,
+    back_out,
+    back_in,
     share,
     coef,
     zh,
     yh,
     pack,
     spread,
-    acc,
     hist_sem,
     sp_sem,
-    send_sem,
-    recv_sem,
+    go_send,
+    go_recv,
+    back_send,
+    back_recv,
     share_send,
     share_recv,
     halo_send,
@@ -93,8 +86,8 @@
 
     after, before = (me + 1) % GROUPS, (me + GROUPS - 1) % GROUPS
     barrier = pltpu.get_barrier_semaphore()
-    for peer in (at(0, 1), at(0, -1), at(1, 0), at(-1, 0), after, before):
-        pl.semaphore_signal(barrier, inc=1, device_id={"stream": peer}, device_id_type=MESH)
+    for d in range(1, GROUPS):
+        pl.semaphore_signal(barrier, inc=1, device_id={"stream": (me + d) % GROUPS}, device_id_type=MESH)
     for d in range(1, spans):
 
         @pl.when(mp + d < spans)
@@ -116,45 +109,18 @@
     coef[7] = count_b
     coef[8] = 1.0 / jnp.maximum(count_b, 1.0)
 
+    def place(s, c):
+        return s // 4, pl.ds(pl.multiple_of(32 * ((s + me) % 4) + 8 * c, 8), 8)
+
     cell_of = jnp.broadcast_to(tile + (128 * me).astype(F32), (32, 128))
-    mine = iota((8, 128), 1) % 8 == iota((8, 128), 0)
     for c in range(CHUNKS):
-        rate[c, me, 8 * NS : ROWS, :] = jnp.sum(jnp.where(mine, cell_of[8 * c : 8 * c + 8], 0.0), axis=0, keepdims=True)
+        block, rows = place(NS, c)
+        rate[block, rows, :] = cell_of[8 * c : 8 * c + 8]
+        for s in (10, 11):
+            block, rows = place(s, c)
+            rate[block, rows, :] = jnp.zeros((8, 128), F32)
     lane32 = iota((32, 128), 1).astype(F32)
     share[mp] = jnp.sum(jnp.where(owner == lane32, count_b, 0.0), axis=0, keepdims=True)
-
-    def send_chunk(c, src, dst):
-        pltpu.make_async_remote_copy(
-            src_ref=rate.at[c, src],
-            dst_ref=rate.at[c, src],
-            send_sem=send_sem,
-            recv_sem=recv_sem.at[c, src],
-            device_id={"stream": dst},
-            device_id_type=MESH,
-        ).start()
-
-    def step_to(c, first, second):
-        return at(second, first) if c < 2 else at(first, second)
-
-    def forward(c, df, dg):
-        src = step_to(c, -df, -dg)
-        e = sign(c)
-        if dg == 0:
-            if df == 0:
-                send_chunk(c, src, step_to(c, e, 0))
-                send_chunk(c, src, step_to(c, -e, 0))
-            elif df == e:
-                send_chunk(c, src, step_to(c, e, 0))
-            send_chunk(c, src, step_to(c, 0, e))
-            send_chunk(c, src, step_to(c, 0, -e))
-        elif dg == e:
-            send_chunk(c, src, step_to(c, 0, e))
-
-    def arrive(c, df, dg):
-        if (df, dg) != (0, 0):
-            src = step_to(c, -df, -dg)
-            pltpu.make_async_copy(rate.at[c, src], rate.at[c, src], recv_sem.at[c, src]).wait()
-            forward(c, df, dg)
 
     def chemistry(c):
         rows = slice(8 * c, 8 * c + 8)
@@ -178,25 +144,32 @@
 
         _, _, _, last = lax.fori_loop(0, SUBMAX, substep, (h1, h2, h3, h1))
         for s in range(NS):
-            rate[c, me, 8 * s : 8 * s + 8, :] = (last[s] - hist[0, s, rows, :]) * inv
+            block, spot = place(s, c)
+            rate[block, spot, :] = (last[s] - hist[0, s, rows, :]) * inv
 
     hist_copy.wait()
-    chemistry(ORDER[0])
+    for c in range(CHUNKS):
+        chemistry(c)
+    for b in range(3):
+        go_out[:, b] = jnp.transpose(rate[b]).reshape(GROUPS, 8, 128)
+    pl.semaphore_wait(barrier, GROUPS - 1 + mp)
+
+    def send(source, target, dst, out_sem, in_sem):
+        pltpu.make_async_remote_copy(
+            src_ref=source.at[dst],
+            dst_ref=target.at[me],
+            send_sem=out_sem,
+            recv_sem=in_sem.at[me],
+            device_id={"stream": dst},
+            device_id_type=MESH,
+        ).start()
+
+    peers = [at(dy, dx) for dy, dx in STEPS]
+    for peer in peers[:-1]:
+        send(go_out, go_in, peer, go_send, go_recv)
+    go_in[me] = go_out[me]
+
     sp_copy.wait()
-    lane = iota((8, 16, 128), 2)
-    packed = jnp.zeros((8, 16, 128), F32)
-    for s in range(NS):
-        turned = pltpu.roll(sp[s], 2 * s + 2, 2)
-        packed = jnp.where((lane == 2 * s + 1) | (lane == 2 * s + 2), turned, packed)
-    pack[...] = packed
-    chemistry(ORDER[1])
-    chemistry(ORDER[2])
-    pl.semaphore_wait(barrier, 6 + mp)
-    for c in ORDER[:3]:
-        forward(c, 0, 0)
-    chemistry(ORDER[3])
-    forward(ORDER[3], 0, 0)
-
     z_halo = [
         pltpu.make_async_remote_copy(
             sp.at[:, 7], zh.at[0], halo_send.at[0], halo_recv.at[0], device_id={"stream": after}, device_id_type=MESH
@@ -207,6 +180,12 @@
     ]
     for copy in z_halo:
         copy.start()
+    lane = iota((8, 16, 128), 2)
+    packed = jnp.zeros((8, 16, 128), F32)
+    for s in range(NS):
+        turned = pltpu.roll(sp[s], 2 * s + 2, 2)
+        packed = jnp.where((lane == 2 * s + 1) | (lane == 2 * s + 2), turned, packed)
+    pack[...] = packed
 
     def send_share(dst):
         pltpu.make_async_remote_copy(
@@ -234,54 +213,55 @@
         def _():
             send_share(mp - d)
 
-    cell = iota((128, 128), 0) + 128 * me
-    cell_z = (cell // 16).astype(F32)
-    cell_x = (cell % 16).astype(F32)
-    lane2 = iota((1, 128), 1)
-
-    def gauss(other):
-        offset = (cell_z - other) * (1.0 / 16.0)
-        return jnp.exp(-0.5 * offset * offset)
-
-    norm = 1.0 / jnp.sum(gauss(iota((128, 128), 1).astype(F32)), axis=1, keepdims=True)
-
-    def filter_part(slots, initial):
-        refs = [(c, step_to(c, -df, -dg)) for c, df, dg in slots]
-        cells = jnp.zeros((1, 128), F32)
-        for k, (c, src) in enumerate(refs):
-            cells = jnp.where(lane2 // 8 == k, rate[c, src, 8 * NS : ROWS, :], cells)
-        z = jnp.floor(cells * (1.0 / 16.0))
-        x = cells - 16.0 * z
-        weight = jnp.where(cell_x == x, gauss(z) * norm, 0.0)
+    for peer in peers[:-1]:
+        pltpu.make_async_copy(go_in.at[peer], go_in.at[peer], go_recv.at[peer]).wait()
+    quarter = iota((8, 128), 1) // 32
+
+    def gathered(s, q):
+        block, k = s // 4, s % 4
+        value = go_in[4 * q, block]
+        for i in range(1, 4):
+            value = jnp.where(quarter == (k + i) % 4, go_in[4 * q + i, block], value)
+        return value if k == 0 else pltpu.roll(value, 128 - 32 * k, 1)
+
+    def line(s):
+        return jnp.concatenate([gathered(s, q) for q in range(4)], axis=1)
+
+    values = [line(s) for s in range(NS)]
+    power = values[0] * values[0]
+    for s in range(1, NS):
+        power = power + values[s] * values[s]
+    power = power * (1.0 / NS)
+    values = jnp.concatenate(values + [power / (power + 1.0)], axis=0)
+    high = values.astype(BF16)
+    low = (values - high.astype(F32)).astype(BF16)
+    left = jnp.concatenate([high, low, high], axis=1)
+
+    cells = line(NS)[0:1]
+    from_z = jnp.floor(cells * (1.0 / 16.0))
+    from_x = cells - 16.0 * from_z
+    row = iota((128, 512), 0)
+    row_z = (row // 16).astype(F32) * (1.0 / 16.0)
+    same_x = (row % 16).astype(F32) == from_x
+    from_z = from_z * (1.0 / 16.0)
+
+    def weights(dst):
+        offset = row_z - (from_z - 0.5 * dst.astype(F32))
+        weight = jnp.where(same_x, jnp.exp(-0.5 * offset * offset), 0.0)
         high = weight.astype(BF16)
         low = (weight - high.astype(F32)).astype(BF16)
-        left = jnp.concatenate([high, high, low], axis=1)
-
-        def split(values):
-            high = values.astype(BF16)
-            low = (values - high.astype(F32)).astype(BF16)
-            return jnp.concatenate([high, low, high], axis=0)
-
-        values = [jnp.concatenate([rate[c, src, 8 * s : 8 * s + 8, :] for c, src in refs], axis=0) for s in range(NS)]
-        power = values[0] * values[0]
-        for s in range(1, NS):
-            power = power + values[s] * values[s]
-        power = power * (1.0 / NS)
-        values = [power / (power + 1.0)] + values
-        for k in range(5):
-            right = jnp.concatenate([split(values[2 * k]), split(values[2 * k + 1])], axis=1)
-            part = jnp.dot(left, right, preferred_element_type=F32)
-            if not initial:
-                part = part + acc[k]
-            acc[k] = part
-
-    events = arrivals()
-    for event in events[:16]:
-        arrive(*event)
-    filter_part(events[:16], True)
-    for event in events[16:32]:
-        arrive(*event)
-    filter_part(events[16:32], False)
+        return jnp.concatenate([high, high, low], axis=1)
+
+    for n in range(0, GROUPS, 2):
+        right = jnp.concatenate([weights(dst) for dst in peers[n : n + 2]], axis=0)
+        part = lax.dot_general(left, right, (((1,), (1,)), ((), ())), preferred_element_type=F32)
+        for k, dst in enumerate(peers[n : n + 2]):
+            piece = part[:, 128 * k : 128 * k + 128]
+            if n + k < GROUPS - 1:
+                back_out[dst] = piece
+                send(back_out, back_in, dst, back_send, back_recv)
+            else:
+                back_in[me] = piece
 
     @pl.when(mp < spans - 1)
     def _():
@@ -294,10 +274,6 @@
         def _():
             wait_share(share_recv, mp + d)
             send_share(mp + d)
-
-    for event in events[32:48]:
-        arrive(*event)
-    filter_part(events[32:48], False)
 
     for copy in z_halo:
         copy.wait()
@@ -344,6 +320,7 @@
         def _():
             wait_share(share_send, mp + d)
 
+    lane2 = iota((1, 128), 1)
     owed = share[0]
     for g in range(1, spans):
         owed = owed + share[g]
@@ -360,22 +337,28 @@
         peaks.append(jnp.where(kind == 0, 1.5, jnp.where(kind == 1, 4.0, jnp.where(kind == 2, 9.0, 19.0))))
     peak = jnp.concatenate(peaks, axis=0).astype(F32)
 
-    for event in events[48:]:
-        arrive(*event)
-    filter_part(events[48:], False)
-
-    thick = 1.0 + peak * acc[0, :, 0:128]
+    cell_z = (iota((128, 128), 0) // 16 + 8 * me).astype(F32)
+    offset = (cell_z - iota((128, 128), 1).astype(F32)) * (1.0 / 16.0)
+    norm = 1.0 / jnp.sum(jnp.exp(-0.5 * offset * offset), axis=1, keepdims=True)
+    peak = peak * norm
+    norm = 4.0 * norm
+
+    for peer in peers[:-1]:
+        pltpu.make_async_copy(back_in.at[peer], back_in.at[peer], back_recv.at[peer]).wait()
+
+    def smoothed(s):
+        return jnp.transpose(back_in[:, 8 * s : 8 * s + 8, :].reshape(128, 128))
+
+    thick = 1.0 + peak * smoothed(NS)
     stretch = 0.02 * thick
-    damp = 4.0 / thick
+    damp = norm / thick
     for s in range(NS):
-        k, half = (s + 1) // 2, (s + 1) % 2
-        fine = acc[k, :, 128 * half : 128 * half + 128]
-        value = sp[s].reshape(128, 128) + stretch * spread[s].reshape(128, 128) + fine * damp
+        value = sp[s].reshape(128, 128) + stretch * spread[s].reshape(128, 128) + smoothed(s) * damp
         out[s] = value.reshape(8, 16, 128)
     load_copy.wait()
-    for c in range(CHUNKS):
-        sent = rate.at[c, pl.ds(0, GROUPS - 1)]
-        pltpu.make_async_copy(sent, sent, send_sem).wait()
+    for buffer, sem in ((go_out, go_send), (back_out, back_send)):
+        sent = buffer.at[pl.ds(0, GROUPS - 1)]
+        pltpu.make_async_copy(sent, sent, sem).wait()
 
 
 def deliver(out, load, out_hbm, load_hbm, sems):
@@ -406,18 +389,23 @@
             pltpu.VMEM((1, 1), jnp.int32),
             pltpu.VMEM((3, NS, 32, 128), F32),
             pltpu.VMEM((NS, 8, 16, 128), F32),
-            pltpu.VMEM((CHUNKS, GROUPS, ROWS, 128), F32),
+            pltpu.VMEM((3, 128, 128), F32),
+            pltpu.VMEM((GROUPS, 3, 8, 128), F32),
+            pltpu.VMEM((GROUPS, 3, 8, 128), F32),
+            pltpu.VMEM((GROUPS, 80, 128), F32),
+            pltpu.VMEM((GROUPS, 80, 128), F32),
             pltpu.VMEM((spans, 1, 128), F32),
             pltpu.VMEM((9, 32, 128), F32),
             pltpu.VMEM((2, NS, 16, 128), F32),
             pltpu.VMEM((2, 8, 16, 128), F32),
             pltpu.VMEM((8, 16, 128), F32),
             pltpu.VMEM((NS, 8, 16, 128), F32),
-            pltpu.VMEM((5, 128, 256), F32),
             pltpu.SemaphoreType.DMA,
             pltpu.SemaphoreType.DMA,
             pltpu.SemaphoreType.DMA,
-            pltpu.SemaphoreType.DMA((CHUNKS, GROUPS)),
+            pltpu.SemaphoreType.DMA((GROUPS,)),
+            pltpu.SemaphoreType.DMA,
+            pltpu.SemaphoreType.DMA((GROUPS,)),
             pltpu.SemaphoreType.DMA((spans,)),
             pltpu.SemaphoreType.DMA((spans,)),
             pltpu.SemaphoreType.DMA((4,)),

time: 28.6 us -> 26.1 us (0.913)
  the two profiles are of different devices: /device:TPU:4 before, /device:TPU:1 now
where the time goes in v3:
time: 26.1 us; the launch traced here: 25.9 us
  Pallas kernels  25.3 us (97%)
  between operations  0.64 us (2%)
    pallas_call x1, Pallas kernels, shards(): pl.pallas_call(functools.partial(kernel, spans), out_shape=(pltpu.VMEM(sp...  23.9 us
    pallas_call x1, Pallas kernels, shards(): pl.pallas_call(deliver, out_shape=results, in_specs=[anywhere, anywhere],...  1.39 us

profile of v3, /device:TPU:1, one launch (start us, length us, event | category | flops | bytes accessed | tf_op | source)
XLA Modules:
  0.0 25.9 jit_solution(1836814511918253859)
XLA Ops:
  0.6 23.9 %shard_map.95 = (f32[9,8,16,128]{3,2,1,0:T(8,128)S(1)}, s32[1,1]{1,0:T(1,128)}) custom-call(f32[9,9]{1,0:T(8,128)} %mech.1, f32[9,8,16,128]{3,2,1,0:T(8,128)} %species_hbm.1, f32[3,9,32,128]{3,2,1,0:T(8,128)} %bitcast.10, s32[1,32]{1,0:T(1,128)} %bitcast.12, s32[1,32]{1,0:T(1,128)} %bitcast.13, s32[1,32]{1,0:T(1,128)} %bitcast.14, s32[1,32]{1,0:T(1,128)} %bitcast.15, ...), custom_call_target="tpu_custom_call" | custom-call | tf_op jit(solution)/shard_map/pallas_call | solution.py:383
  24.6 1.4 %shard_map.96 = (f32[9,8,16,128]{3,2,1,0:T(8,128)}, s32[1,1]{1,0:T(1,128)}) custom-call(f32[9,8,16,128]{3,2,1,0:T(8,128)S(1)} %get-tuple-element.4.out, s32[1,1]{1,0:T(1,128)} %get-tuple-element.5.load), custom_call_target="tpu_custom_call" | custom-call | tf_op jit(solution)/shard_map/pallas_call | solution.py:427

commit v4 on v3

--- a/solution.py
+++ b/solution.py
@@ -15,10 +15,8 @@
 SIDE = 4
 GROUPS = SIDE * SIDE
 CHUNKS = 4
-STEPS = (
-    (2, 2), (1, 2), (2, 1), (3, 2), (2, 3), (1, 1), (3, 3), (1, 3),
-    (3, 1), (0, 2), (2, 0), (0, 1), (1, 0), (0, 3), (3, 0), (0, 0),
-)
+FIRST = ((2, 2), (1, 2), (2, 1), (3, 2), (2, 3), (1, 1), (3, 3), (0, 0))
+OTHERS = ((1, 3), (3, 1), (0, 2), (2, 0), (0, 1), (1, 0), (0, 3), (3, 0))
 
 
 def iota(shape, dim):
@@ -37,20 +35,27 @@
 
 def kernel(
     spans,
-    mech,
+    mech_hbm,
     species_hbm,
     history_hbm,
+    tiles_hbm,
+    owners_hbm,
+    orders_hbm,
+    steps_hbm,
+    levels_hbm,
+    out,
+    mech,
     tiles,
     owners,
     orders,
     steps,
     levels,
-    out,
-    load_out,
-    load,
     hist,
     sp,
     rate,
+    meta,
+    wts,
+    left,
     go_out,
     go_in,
     back_out,
@@ -61,8 +66,11 @@
     yh,
     pack,
     spread,
+    table_sem,
     hist_sem,
     sp_sem,
+    meta_send,
+    meta_recv,
     go_send,
     go_recv,
     back_send,
@@ -76,6 +84,21 @@
     mp = lax.axis_index("span")
     sy, sx = me // SIDE, me % SIDE
 
+    table_copies = [
+        pltpu.make_async_copy(source, target, table_sem.at[k])
+        for k, (source, target) in enumerate(
+            (
+                (orders_hbm, orders),
+                (steps_hbm, steps),
+                (tiles_hbm, tiles),
+                (owners_hbm, owners),
+                (mech_hbm, mech),
+                (levels_hbm, levels),
+            )
+        )
+    ]
+    for copy in table_copies:
+        copy.start()
     hist_copy = pltpu.make_async_copy(history_hbm, hist, hist_sem)
     hist_copy.start()
     sp_copy = pltpu.make_async_copy(species_hbm, sp, sp_sem)
@@ -94,6 +117,8 @@
         def _():
             pl.semaphore_signal(barrier, inc=1, device_id={"span": mp + d}, device_id_type=MESH)
 
+    for copy in table_copies:
+        copy.wait()
     order = jnp.broadcast_to(column(orders[...], 32), (32, 128))
     count = column(steps[...], 32)
     tile = column(tiles[...], 32)
@@ -113,10 +138,10 @@
         return s // 4, pl.ds(pl.multiple_of(32 * ((s + me) % 4) + 8 * c, 8), 8)
 
     cell_of = jnp.broadcast_to(tile + (128 * me).astype(F32), (32, 128))
+    mine = iota((32, 128), 1) == iota((32, 128), 0) + 32 * (me % 4)
+    meta[me] = jnp.sum(jnp.where(mine, cell_of, 0.0), axis=0, keepdims=True)
     for c in range(CHUNKS):
-        block, rows = place(NS, c)
-        rate[block, rows, :] = cell_of[8 * c : 8 * c + 8]
-        for s in (10, 11):
+        for s in (9, 10, 11):
             block, rows = place(s, c)
             rate[block, rows, :] = jnp.zeros((8, 128), F32)
     lane32 = iota((32, 128), 1).astype(F32)
@@ -127,10 +152,10 @@
         p1, p2, p3, a1, a2, a3, hb, cnt, inv = [coef[k, rows, :] for k in range(9)]
         h1, h2, h3 = [tuple(hist[m, s, rows, :] for s in range(NS)) for m in range(3)]
 
-        def substep(n, carry):
-            h1, h2, h3, last = carry
+        last = h1
+        for n in range(SUBMAX):
             guess = [p1 * h1[s] + p2 * h2[s] + p3 * h3[s] for s in range(NS)]
-            active = cnt > n.astype(F32)
+            active = cnt > F32(n)
             fresh = []
             done = []
             for s in range(NS):
@@ -140,9 +165,7 @@
                 y = a1 * h1[s] + a2 * h2[s] + a3 * h3[s] + hb * jnp.tanh(total)
                 fresh.append(y)
                 done.append(jnp.where(active, y, last[s]))
-            return tuple(fresh), h1, h2, tuple(done)
-
-        _, _, _, last = lax.fori_loop(0, SUBMAX, substep, (h1, h2, h3, h1))
+            h1, h2, h3, last = fresh, h1, h2, done
         for s in range(NS):
             block, spot = place(s, c)
             rate[block, spot, :] = (last[s] - hist[0, s, rows, :]) * inv
@@ -156,17 +179,21 @@
 
     def send(source, target, dst, out_sem, in_sem):
         pltpu.make_async_remote_copy(
-            src_ref=source.at[dst],
+            src_ref=source,
             dst_ref=target.at[me],
             send_sem=out_sem,
-            recv_sem=in_sem.at[me],
+            recv_sem=in_sem,
             device_id={"stream": dst},
             device_id_type=MESH,
         ).start()
 
-    peers = [at(dy, dx) for dy, dx in STEPS]
-    for peer in peers[:-1]:
-        send(go_out, go_in, peer, go_send, go_recv)
+    first = [at(dy, dx) for dy, dx in FIRST]
+    others = [at(dy, dx) for dy, dx in OTHERS]
+    peers = first[:-1] + others
+    for peer in peers:
+        send(meta.at[me], meta, peer, meta_send, meta_recv)
+    for peer in peers:
+        send(go_out.at[peer], go_in, peer, go_send, go_recv.at[me])
     go_in[me] = go_out[me]
 
     sp_copy.wait()
@@ -213,7 +240,27 @@
         def _():
             send_share(mp - d)
 
-    for peer in peers[:-1]:
+    some = meta.at[pl.ds(0, GROUPS - 1)]
+    pltpu.make_async_copy(some, some, meta_recv).wait()
+    cells = jnp.concatenate([meta[4 * q] + meta[4 * q + 1] + meta[4 * q + 2] + meta[4 * q + 3] for q in range(4)], axis=1)
+    from_z = jnp.floor(cells * (1.0 / 16.0))
+    from_x = cells - 16.0 * from_z
+    row = iota((128, 512), 0)
+    row_z = (row // 16).astype(F32) * (1.0 / 16.0)
+    same_x = (row % 16).astype(F32) == from_x
+    from_z = from_z * (1.0 / 16.0)
+
+    def weights(dst):
+        offset = row_z - (from_z - 0.5 * dst.astype(F32))
+        weight = jnp.where(same_x, jnp.exp(-0.5 * offset * offset), 0.0)
+        high = weight.astype(BF16)
+        low = (weight - high.astype(F32)).astype(BF16)
+        return jnp.concatenate([high, high, low], axis=1)
+
+    for n, dst in enumerate(first):
+        wts[n] = weights(dst)
+
+    for peer in peers:
         pltpu.make_async_copy(go_in.at[peer], go_in.at[peer], go_recv.at[peer]).wait()
     quarter = iota((8, 128), 1) // 32
 
@@ -224,10 +271,7 @@
             value = jnp.where(quarter == (k + i) % 4, go_in[4 * q + i, block], value)
         return value if k == 0 else pltpu.roll(value, 128 - 32 * k, 1)
 
-    def line(s):
-        return jnp.concatenate([gathered(s, q) for q in range(4)], axis=1)
-
-    values = [line(s) for s in range(NS)]
+    values = [jnp.concatenate([gathered(s, q) for q in range(4)], axis=1) for s in range(NS)]
     power = values[0] * values[0]
     for s in range(1, NS):
         power = power + values[s] * values[s]
@@ -235,33 +279,39 @@
     values = jnp.concatenate(values + [power / (power + 1.0)], axis=0)
     high = values.astype(BF16)
     low = (values - high.astype(F32)).astype(BF16)
-    left = jnp.concatenate([high, low, high], axis=1)
-
-    cells = line(NS)[0:1]
-    from_z = jnp.floor(cells * (1.0 / 16.0))
-    from_x = cells - 16.0 * from_z
-    row = iota((128, 512), 0)
-    row_z = (row // 16).astype(F32) * (1.0 / 16.0)
-    same_x = (row % 16).astype(F32) == from_x
-    from_z = from_z * (1.0 / 16.0)
-
-    def weights(dst):
-        offset = row_z - (from_z - 0.5 * dst.astype(F32))
-        weight = jnp.where(same_x, jnp.exp(-0.5 * offset * offset), 0.0)
-        high = weight.astype(BF16)
-        low = (weight - high.astype(F32)).astype(BF16)
-        return jnp.concatenate([high, high, low], axis=1)
-
-    for n in range(0, GROUPS, 2):
-        right = jnp.concatenate([weights(dst) for dst in peers[n : n + 2]], axis=0)
-        part = lax.dot_general(left, right, (((1,), (1,)), ((), ())), preferred_element_type=F32)
-        for k, dst in enumerate(peers[n : n + 2]):
-            piece = part[:, 128 * k : 128 * k + 128]
-            if n + k < GROUPS - 1:
-                back_out[dst] = piece
-                send(back_out, back_in, dst, back_send, back_recv)
-            else:
-                back_in[me] = piece
+    left[...] = jnp.concatenate([high, low, high], axis=1)
+
+    def product(right):
+        return lax.dot_general(left[...], right, (((1,), (1,)), ((), ())), preferred_element_type=F32)
+
+    def give(piece, dst):
+        back_out[dst] = piece
+        send(back_out.at[dst], back_in, dst, back_send, back_recv.at[me])
+
+    for n in range(0, 8, 2):
+        part = product(wts[n : n + 2].reshape(256, 1536))
+        give(part[:, :128], first[n])
+        if n + 1 < 7:
+            give(part[:, 128:], first[n + 1])
+        else:
+            back_in[me] = part[:, 128:]
+
+    steps_y = sum(dy << (2 * k) for k, (dy, _) in enumerate(OTHERS))
+    steps_x = sum(dx << (2 * k) for k, (_, dx) in enumerate(OTHERS))
+
+    def two_others(n, _):
+        pair = []
+        for k in range(2):
+            shift = 4 * n + 2 * k
+            dy = lax.shift_right_logical(jnp.int32(steps_y), shift) & 3
+            dx = lax.shift_right_logical(jnp.int32(steps_x), shift) & 3
+            pair.append(at(dy, dx))
+        part = product(jnp.concatenate([weights(dst) for dst in pair], axis=0))
+        for k, dst in enumerate(pair):
+            give(part[:, 128 * k : 128 * k + 128], dst)
+        return 0
+
+    lax.fori_loop(0, 4, two_others, 0)
 
     @pl.when(mp < spans - 1)
     def _():
@@ -325,9 +375,7 @@
     for g in range(1, spans):
         owed = owed + share[g]
     here = jnp.where(lane2 == mp, owed, 0.0)
-    load[...] = jnp.sum(here, axis=1, keepdims=True).astype(jnp.int32)
-    load_copy = pltpu.make_async_copy(load, load_out, hist_sem)
-    load_copy.start()
+    out[8 * NS] = jnp.broadcast_to(jnp.sum(here, axis=1, keepdims=True), (16, 128))
 
     peaks = []
     for z in range(8):
@@ -343,7 +391,7 @@
     peak = peak * norm
     norm = 4.0 * norm
 
-    for peer in peers[:-1]:
+    for peer in peers:
         pltpu.make_async_copy(back_in.at[peer], back_in.at[peer], back_recv.at[peer]).wait()
 
     def smoothed(s):
@@ -354,20 +402,21 @@
     damp = norm / thick
     for s in range(NS):
         value = sp[s].reshape(128, 128) + stretch * spread[s].reshape(128, 128) + smoothed(s) * damp
-        out[s] = value.reshape(8, 16, 128)
-    load_copy.wait()
-    for buffer, sem in ((go_out, go_send), (back_out, back_send)):
+        out[8 * s : 8 * s + 8] = value.reshape(8, 16, 128)
+    for buffer, sem in ((meta, meta_send), (go_out, go_send), (back_out, back_send)):
         sent = buffer.at[pl.ds(0, GROUPS - 1)]
         pltpu.make_async_copy(sent, sent, sem).wait()
 
 
-def deliver(out, load, out_hbm, load_hbm, sems):
+def deliver(both, out_hbm, load_hbm, load, sems):
+    cells = both.at[pl.ds(0, 8 * NS)]
     copies = [
-        pltpu.make_async_copy(out, out_hbm, sems.at[0]),
+        pltpu.make_async_copy(cells, out_hbm, sems.at[0]),
         pltpu.make_async_copy(load, load_hbm, sems.at[1]),
     ]
-    for copy in copies:
-        copy.start()
+    copies[0].start()
+    load[...] = both[8 * NS, 0:1, 0:1].astype(jnp.int32)
+    copies[1].start()
     for copy in copies:
         copy.wait()
 
@@ -376,20 +425,24 @@
     states = jnp.transpose(history, (0, 1, 3, 4, 2, 5)).reshape(3, NS, 32, 128)
     vmem = pl.BlockSpec(memory_space=pltpu.VMEM)
     anywhere = pl.BlockSpec(memory_space=pl.ANY)
-    results = (
-        jax.ShapeDtypeStruct(species.shape, F32),
-        jax.ShapeDtypeStruct((1, 1), jnp.int32),
-    )
-    out, load = pl.pallas_call(
+    both = pl.pallas_call(
         functools.partial(kernel, spans),
-        out_shape=(pltpu.VMEM(species.shape, F32), results[1]),
-        in_specs=[pl.BlockSpec(memory_space=pltpu.SMEM), anywhere, anywhere] + [vmem] * 5,
-        out_specs=(vmem, anywhere),
+        out_shape=pltpu.VMEM((8 * NS + 1, 16, 128), F32),
+        in_specs=[anywhere] * 8,
+        out_specs=vmem,
         scratch_shapes=[
-            pltpu.VMEM((1, 1), jnp.int32),
+            pltpu.SMEM((NS, NS), F32),
+            pltpu.VMEM((1, 32), jnp.int32),
+            pltpu.VMEM((1, 32), jnp.int32),
+            pltpu.VMEM((1, 32), jnp.int32),
+            pltpu.VMEM((1, 32), jnp.int32),
+            pltpu.VMEM((8, 1, 16), jnp.int32),
             pltpu.VMEM((3, NS, 32, 128), F32),
             pltpu.VMEM((NS, 8, 16, 128), F32),
             pltpu.VMEM((3, 128, 128), F32),
+            pltpu.VMEM((GROUPS, 1, 128), F32),
+            pltpu.VMEM((8, 128, 1536), BF16),
+            pltpu.VMEM((80, 1536), BF16),
             pltpu.VMEM((GROUPS, 3, 8, 128), F32),
             pltpu.VMEM((GROUPS, 3, 8, 128), F32),
             pltpu.VMEM((GROUPS, 80, 128), F32),
@@ -400,6 +453,9 @@
             pltpu.VMEM((2, 8, 16, 128), F32),
             pltpu.VMEM((8, 16, 128), F32),
             pltpu.VMEM((NS, 8, 16, 128), F32),
+            pltpu.SemaphoreType.DMA((6,)),
+            pltpu.SemaphoreType.DMA,
+            pltpu.SemaphoreType.DMA,
             pltpu.SemaphoreType.DMA,
             pltpu.SemaphoreType.DMA,
             pltpu.SemaphoreType.DMA,
@@ -424,14 +480,18 @@
         substeps.reshape(1, 32),
         jnp.transpose(levels, (0, 2, 1)),
     )
-    return pl.pallas_call(
+    out, load = pl.pallas_call(
         deliver,
-        out_shape=results,
-        in_specs=[anywhere, anywhere],
+        out_shape=(
+            jax.ShapeDtypeStruct((8 * NS, 16, 128), F32),
+            jax.ShapeDtypeStruct((1, 1), jnp.int32),
+        ),
+        in_specs=[vmem],
         out_specs=(anywhere, anywhere),
-        scratch_shapes=[pltpu.SemaphoreType.DMA((2,))],
+        scratch_shapes=[pltpu.VMEM((1, 1), jnp.int32), pltpu.SemaphoreType.DMA((2,))],
         compiler_params=pltpu.CompilerParams(vmem_limit_bytes=2**20),
-    )(out, load)
+    )(both)
+    return out.reshape(species.shape), load
 
 
 def solution(mesh):

time: 26.1 us -> 24.7 us (0.946)
  Pallas kernels: 25.3 us -> 24 us
    pallas_call x2, Pallas kernels: 25.3 us -> 24 us  [the longest x1 23.1 us: shards(): pl.pallas_call(functools.partial(kernel, spans), out_shape=pltpu.VMEM((8...]
where the time goes in v4:
time: 24.7 us; the launch traced here: 24.6 us
  Pallas kernels  24 us (97%)
  between operations  0.64 us (3%)
    pallas_call x1, Pallas kernels, shards(): pl.pallas_call(functools.partial(kernel, spans), out_shape=pltpu.VMEM((8...  23.1 us
    pallas_call x1, Pallas kernels, shards(): pl.pallas_call(deliver, out_shape=(jax.ShapeDtypeStruct((8 * NS, 16, 128)...  0.84 us

profile of v4, /device:TPU:1, one launch (start us, length us, event | category | flops | bytes accessed | tf_op | source)
XLA Modules:
  0.0 24.6 jit_solution(16762525308487820594)
XLA Ops:
  0.6 23.1 %shard_map.95.both = f32[73,16,128]{2,1,0:T(8,128)S(1)} custom-call(f32[9,9]{1,0:T(8,128)} %mech_hbm.1, f32[9,8,16,128]{3,2,1,0:T(8,128)} %species_hbm.1, f32[3,9,32,128]{3,2,1,0:T(8,128)} %bitcast.11, s32[1,32]{1,0:T(1,128)} %bitcast.13, s32[1,32]{1,0:T(1,128)} %bitcast.14, s32[1,32]{1,0:T(1,128)} %bitcast.15, s32[1,32]{1,0:T(1,128)} %bitcast.16, ...), custom_call_target="tpu_custom_call" | custom-call | tf_op jit(solution)/shard_map/pallas_call | solution.py:428
  23.8 0.8 %shard_map.96 = (f32[72,16,128]{2,1,0:T(8,128)}, s32[1,1]{1,0:T(1,128)}) custom-call(f32[73,16,128]{2,1,0:T(8,128)S(1)} %shard_map.95.both), custom_call_target="tpu_custom_call" | custom-call | tf_op jit(solution)/shard_map/pallas_call | solution.py:483

commit v5 on v4

--- a/solution.py
+++ b/solution.py
@@ -15,8 +15,8 @@
 SIDE = 4
 GROUPS = SIDE * SIDE
 CHUNKS = 4
-FIRST = ((2, 2), (1, 2), (2, 1), (3, 2), (2, 3), (1, 1), (3, 3), (0, 0))
-OTHERS = ((1, 3), (3, 1), (0, 2), (2, 0), (0, 1), (1, 0), (0, 3), (3, 0))
+FIRST = ((1, 1), (3, 3), (2, 0), (3, 1), (1, 3), (2, 2), (2, 1), (0, 0))
+OTHERS = ((2, 3), (1, 0), (1, 2), (3, 2), (3, 0), (0, 2), (0, 1), (0, 3))
 
 
 def iota(shape, dim):

time: 24.7 us -> 23.2 us (0.939); the launches traced: 24.6 us -> 22.8 us
  Pallas kernels: 24 us -> 22.1 us
    pallas_call x1, Pallas kernels: 23.1 us -> 21.3 us  [shards(): pl.pallas_call(functools.partial(kernel, spans), out_shape=pltpu.VMEM((8...]
where the time goes in v5:
time: 23.2 us; the launch traced here: 22.8 us
  Pallas kernels  22.1 us (95%)
  between operations  0.64 us (3%)
    pallas_call x1, Pallas kernels, shards(): pl.pallas_call(functools.partial(kernel, spans), out_shape=pltpu.VMEM((8...  21.3 us
    pallas_call x1, Pallas kernels, shards(): pl.pallas_call(deliver, out_shape=(jax.ShapeDtypeStruct((8 * NS, 16, 128)...  0.84 us

profile of v5, /device:TPU:1, one launch (start us, length us, event | category | flops | bytes accessed | tf_op | source)
XLA Modules:
  0.0 22.8 jit_solution(12930339002338576026)
XLA Ops:
  0.6 21.3 %shard_map.95.both = f32[73,16,128]{2,1,0:T(8,128)S(1)} custom-call(f32[9,9]{1,0:T(8,128)} %mech_hbm.1, f32[9,8,16,128]{3,2,1,0:T(8,128)} %species_hbm.1, f32[3,9,32,128]{3,2,1,0:T(8,128)} %bitcast.11, s32[1,32]{1,0:T(1,128)} %bitcast.13, s32[1,32]{1,0:T(1,128)} %bitcast.14, s32[1,32]{1,0:T(1,128)} %bitcast.15, s32[1,32]{1,0:T(1,128)} %bitcast.16, ...), custom_call_target="tpu_custom_call" | custom-call | tf_op jit(solution)/shard_map/pallas_call | solution.py:428
  21.9 0.8 %shard_map.96 = (f32[72,16,128]{2,1,0:T(8,128)}, s32[1,1]{1,0:T(1,128)}) custom-call(f32[73,16,128]{2,1,0:T(8,128)S(1)} %shard_map.95.both), custom_call_target="tpu_custom_call" | custom-call | tf_op jit(solution)/shard_map/pallas_call | solution.py:483

commit v6 on v5

--- a/solution.py
+++ b/solution.py
@@ -16,7 +16,7 @@
 GROUPS = SIDE * SIDE
 CHUNKS = 4
 FIRST = ((1, 1), (3, 3), (2, 0), (3, 1), (1, 3), (2, 2), (2, 1), (0, 0))
-OTHERS = ((2, 3), (1, 0), (1, 2), (3, 2), (3, 0), (0, 2), (0, 1), (0, 3))
+OTHERS = ((2, 3), (1, 2), (3, 2), (1, 0), (3, 0), (0, 2), (0, 3), (0, 1))
 
 
 def iota(shape, dim):

time: 23.2 us -> 23 us (level)
  no operation moved by 1% of the time
where the time goes in v6:
time: 23 us; the launch traced here: 22.8 us
  Pallas kernels  22.2 us (97%)
  between operations  0.64 us (3%)
    pallas_call x1, Pallas kernels, shards(): pl.pallas_call(functools.partial(kernel, spans), out_shape=pltpu.VMEM((8...  21.3 us
    pallas_call x1, Pallas kernels, shards(): pl.pallas_call(deliver, out_shape=(jax.ShapeDtypeStruct((8 * NS, 16, 128)...  0.84 us

profile of v6, /device:TPU:1, one launch (start us, length us, event | category | flops | bytes accessed | tf_op | source)
XLA Modules:
  0.0 22.8 jit_solution(10599544098643244336)
XLA Ops:
  0.6 21.3 %shard_map.95.both = f32[73,16,128]{2,1,0:T(8,128)S(1)} custom-call(f32[9,9]{1,0:T(8,128)} %mech_hbm.1, f32[9,8,16,128]{3,2,1,0:T(8,128)} %species_hbm.1, f32[3,9,32,128]{3,2,1,0:T(8,128)} %bitcast.11, s32[1,32]{1,0:T(1,128)} %bitcast.13, s32[1,32]{1,0:T(1,128)} %bitcast.14, s32[1,32]{1,0:T(1,128)} %bitcast.15, s32[1,32]{1,0:T(1,128)} %bitcast.16, ...), custom_call_target="tpu_custom_call" | custom-call | tf_op jit(solution)/shard_map/pallas_call | solution.py:428
  22.0 0.8 %shard_map.96 = (f32[72,16,128]{2,1,0:T(8,128)}, s32[1,1]{1,0:T(1,128)}) custom-call(f32[73,16,128]{2,1,0:T(8,128)S(1)} %shard_map.95.both), custom_call_target="tpu_custom_call" | custom-call | tf_op jit(solution)/shard_map/pallas_call | solution.py:483

commit v7 on v6

--- a/solution.py
+++ b/solution.py
@@ -109,8 +109,8 @@
 
     after, before = (me + 1) % GROUPS, (me + GROUPS - 1) % GROUPS
     barrier = pltpu.get_barrier_semaphore()
-    for d in range(1, GROUPS):
-        pl.semaphore_signal(barrier, inc=1, device_id={"stream": (me + d) % GROUPS}, device_id_type=MESH)
+    for dy, dx in sorted(FIRST[:-1] + OTHERS, key=lambda step: -(min(step[0], 4 - step[0]) + min(step[1], 4 - step[1]))):
+        pl.semaphore_signal(barrier, inc=1, device_id={"stream": at(dy, dx)}, device_id_type=MESH)
     for d in range(1, spans):
 
         @pl.when(mp + d < spans)

time: 23 us -> 22.9 us (level)
  no operation moved by 1% of the time
where the time goes in v7:
time: 22.9 us; the launch traced here: 22.7 us
  Pallas kernels  22.1 us (97%)
  between operations  0.64 us (3%)
    pallas_call x1, Pallas kernels, shards(): pl.pallas_call(functools.partial(kernel, spans), out_shape=pltpu.VMEM((8...  21.3 us
    pallas_call x1, Pallas kernels, shards(): pl.pallas_call(deliver, out_shape=(jax.ShapeDtypeStruct((8 * NS, 16, 128)...  0.84 us

profile of v7, /device:TPU:1, one launch (start us, length us, event | category | flops | bytes accessed | tf_op | source)
XLA Modules:
  0.0 22.7 jit_solution(11593024188091825940)
XLA Ops:
  0.6 21.3 %shard_map.95.both = f32[73,16,128]{2,1,0:T(8,128)S(1)} custom-call(f32[9,9]{1,0:T(8,128)} %mech_hbm.1, f32[9,8,16,128]{3,2,1,0:T(8,128)} %species_hbm.1, f32[3,9,32,128]{3,2,1,0:T(8,128)} %bitcast.11, s32[1,32]{1,0:T(1,128)} %bitcast.13, s32[1,32]{1,0:T(1,128)} %bitcast.14, s32[1,32]{1,0:T(1,128)} %bitcast.15, s32[1,32]{1,0:T(1,128)} %bitcast.16, ...), custom_call_target="tpu_custom_call" | custom-call | tf_op jit(solution)/shard_map/pallas_call | solution.py:428
  21.9 0.8 %shard_map.96 = (f32[72,16,128]{2,1,0:T(8,128)}, s32[1,1]{1,0:T(1,128)}) custom-call(f32[73,16,128]{2,1,0:T(8,128)S(1)} %shard_map.95.both), custom_call_target="tpu_custom_call" | custom-call | tf_op jit(solution)/shard_map/pallas_call | solution.py:483
